TPU v7x, 32 devices: a whole 2x2x4 slice. The times are simulated.
32 devices in a mesh: elem: 16 (over z, x, core), head: 2 (over y).
Axes of the slice: x: 2, y: 2, z: 4, core: 2. Of those that a mesh axis runs over, the one named last changes fastest.
Arguments:
- features: bfloat16 [16384, 512], P('elem'), may hold values from -6 to 6
- out_grad: bfloat16 [16384, 512], P('elem'), may hold values from -6 to 6
- bin_order: int32 [16384], P('elem'), may hold values from 0 to 16383, as said below
- key_lists: int32 [128, 12], P('elem'), may hold values from 0 to 127, as said below
- list_counts: int32 [128], P('elem'), may hold values from 1 to 12, as said below
- attn_gain: float32 [512], replicated, may hold values from 0.1 to 1.9
- query_weight: bfloat16 [512, 512], P(None, 'head')
- key_weight: bfloat16 [512, 512], P(None, 'head')
- value_weight: bfloat16 [512, 512], P(None, 'head'), may hold values from -0.25 to 0.25
- out_weight: bfloat16 [512, 512], P('head'), may hold values from -0.25 to 0.25
- ffn_gain: float32 [512], replicated, may hold values from 0.1 to 1.9
- ffn_in: bfloat16 [512, 2048], P(None, 'head'), may hold values from -0.25 to 0.25
- ffn_out: bfloat16 [2048, 512], P('head'), may hold values from -0.125 to 0.125
Outputs:
- output: bfloat16 [16384, 512], P('elem', 'head')
- input_grad: float32 [16384, 512], P('elem', 'head')
Inputs may be any that keep to these rules, and one draw needn't show every extreme that they name: `bin_order`: the rows of region e, numbers e * 1024 to (e + 1) * 1024 - 1, hold a permutation of those same numbers. `key_lists`: slot 0 of row b is b; the other slots hold distinct blocks other than b, all of the regions r - 1, r and r + 1 modulo 16, where r = b // 8 and region r holds blocks r * 8 to (r + 1) * 8 - 1; in row r * 8 of every region, slot 1 is a block of region r - 1 and slot 2 a block of region r + 1. list_counts[r * 8] = 12 for every region r.
All inputs are finite; a program needn't handle non-finite values.
Results may differ from a plain program's by a relative error of at most 0.024.
Values may be sent and summed in bfloat16 or wider, within the bound.
No kernel may reach another device: no remote copies, remote signals or barrier semaphores. Data moves between devices by JAX's collectives and lax.ppermute only.
A program may use at most 128 MiB of HBM per device.

v0:
```python
import functools

import jax
import jax.numpy as jnp
from jax import lax
from jax.experimental import pallas as pl
from jax.experimental.pallas import tpu as pltpu
from jax.sharding import PartitionSpec as P

HD = 64
PAIR = 2 * HD
EPSILON = 1e-05
F32 = jnp.float32
BF16 = jnp.bfloat16
VMEM = pl.BlockSpec(memory_space=pltpu.VMEM)
SMEM = pl.BlockSpec(memory_space=pltpu.SMEM)
COUNT_COL = 12
BLOCK_COL = 13
GROUP_COL = 14
OWN_COL = 15
LOW_COL = 16
META_COLS = 128
COST = 1000


def dot_nn(a, b):
    return lax.dot_general(a, b, (((1,), (0,)), ((), ())), preferred_element_type=F32)


def dot_nt(a, b):
    return lax.dot_general(a, b, (((1,), (1,)), ((), ())), preferred_element_type=F32)


def row_scale(values):
    return lax.rsqrt(jnp.mean(values * values, axis=-1, keepdims=True) + EPSILON)


def call(kernel, out_shape, in_specs, scratch=(), vmem=16):
    out_specs = jax.tree.map(lambda _: VMEM, out_shape)
    return pl.pallas_call(
        kernel,
        out_shape=out_shape,
        in_specs=in_specs,
        out_specs=out_specs,
        scratch_shapes=list(scratch),
        compiler_params=pltpu.CompilerParams(vmem_limit_bytes=vmem << 20),
        cost_estimate=pl.CostEstimate(flops=COST, bytes_accessed=COST, transcendentals=0),
    )


def shaped(shape, dtype):
    return jax.ShapeDtypeStruct(shape, dtype)


def column_of(row, size):
    return jnp.broadcast_to(row, (size, size)).T


def sort_matrix(pos_ref, first, size, total):
    lanes = lax.broadcasted_iota(jnp.int32, (128, total), 1).astype(F32)
    parts = []
    for start in range(first, first + size, 128):
        column = column_of(places(pos_ref, start, 128).astype(F32), 128)
        wide = jnp.concatenate([column] * (total // 128), axis=1)
        parts.append(jnp.where(wide == lanes, 1.0, 0.0).astype(BF16))
    return jnp.concatenate(parts, axis=0)


def places(pos_ref, start, size):
    return lax.rem(pos_ref[:, start : start + size], pos_ref.shape[1])


def plan_kernel(head_groups, where_ref, lists_ref, counts_ref, meta_ref):
    blocks, slots = lists_ref.shape
    region, regions, group, heads = where_ref[0], where_ref[1], where_ref[2], head_groups
    counts = [counts_ref[i] for i in range(blocks)]
    for i in range(blocks):
        rank = jnp.int32(0)
        for j in range(blocks):
            if j != i:
                ahead = counts[j] >= counts[i] if j < i else counts[j] > counts[i]
                rank = rank + jnp.where(ahead, 1, 0)
        turn = rank // heads
        side = rank % heads
        side = jnp.where(turn % 2 == 1, heads - 1 - side, side)
        from_me = group - side
        from_me = jnp.where(from_me < 0, from_me + heads, from_me)
        row = from_me * (blocks // heads) + turn
        meta_ref[row, COUNT_COL] = counts[i]
        meta_ref[row, BLOCK_COL] = jnp.int32(i)
        meta_ref[row, GROUP_COL] = group
        entries = []
        own_total = low_total = jnp.int32(0)
        for s in range(slots):
            key = lists_ref[i, s]
            away = key // blocks - region + 1
            away = jnp.where(away < 0, away + regions, away)
            away = jnp.where(away >= regions, away - regions, away)
            entries.append((key % blocks + jnp.where(away == 2, blocks, 0), away))
            live = s < counts[i]
            own_total = own_total + jnp.where((away == 1) & live, 1, 0)
            low_total = low_total + jnp.where((away == 0) & live, 1, 0)
        meta_ref[row, OWN_COL] = own_total
        meta_ref[row, LOW_COL] = low_total
        own_next, low_next, high_next = jnp.int32(0), own_total, own_total + low_total
        for s in range(slots):
            index, away = entries[s]
            to = jnp.where(away == 1, own_next, jnp.where(away == 0, low_next, high_next))

            @pl.when(s < counts[i])
            def _(index=index, to=to):
                meta_ref[row, to] = index

            own_next = own_next + jnp.where(away == 1, 1, 0)
            low_next = low_next + jnp.where(away == 0, 1, 0)
            high_next = high_next + jnp.where(away == 2, 1, 0)


def prep_kernel(pos_ref, rows_ref, gain_ref, normed_ref):
    total = rows_ref.shape[0]
    for first in range(0, total, 512):
        picked = dot_nn(sort_matrix(pos_ref, first, 512, total), rows_ref[...])
        normed_ref[first : first + 512, :] = (picked * row_scale(picked) * gain_ref[...]).astype(BF16)


def sort_kernel(pos_ref, rows_ref, grads_ref, sorted_rows_ref, sorted_grads_ref):
    total = rows_ref.shape[0]
    for first in range(0, total, 512):
        matrix = sort_matrix(pos_ref, first, 512, total)
        sorted_rows_ref[first : first + 512, :] = dot_nn(matrix, rows_ref[...]).astype(BF16)
        sorted_grads_ref[first : first + 512, :] = dot_nn(matrix, grads_ref[...]).astype(BF16)


def chunk(values, who, share):
    out = values[:, :share]
    for start in range(share, values.shape[1], share):
        out = jnp.where(who == start // share, values[:, start : start + share], out)
    return out


def below(group, steps, count):
    who = group + steps
    return jnp.where(who >= count, who - count, who)


def both_heads(rows):
    lane = lax.broadcasted_iota(jnp.int32, rows.shape, 1)
    zero = jnp.zeros_like(rows)
    return jnp.concatenate([jnp.where(lane < HD, rows, zero), jnp.where(lane < HD, zero, rows)], axis=0)


def both_heads_t(rows):
    flipped = rows.T
    row = lax.broadcasted_iota(jnp.int32, flipped.shape, 0)
    zero = jnp.zeros_like(flipped)
    return jnp.concatenate([jnp.where(row < HD, flipped, zero), jnp.where(row < HD, zero, flipped)], axis=1)


def own_heads(wide):
    half = wide.shape[1] // 2
    return jnp.concatenate([wide[:HD, :half], wide[HD:, half:]], axis=0)


def groups_of_eight(tile, op):
    out = tile[:8]
    for start in range(8, tile.shape[0], 8):
        out = op(out, tile[start : start + 8])
    return out


def packed(packs, which):
    size = packs[0].shape[1] // 4
    return jnp.concatenate([ref[:, which * size : (which + 1) * size] for ref in packs], axis=1)


def joined(mine_ref, packs, which):
    return jnp.concatenate([mine_ref[...], packed(packs, which)], axis=1)


def project_keys(rows_ref, wk, wv, keys_ref, values_ref, values_t_ref, base):
    for start in range(0, rows_ref.shape[0], 512):
        at = slice(base + start, base + start + 512)
        here = rows_ref[start : start + 512, :]
        keys_ref[at, :] = dot_nn(here, wk).astype(BF16)
        found = dot_nn(here, wv).astype(BF16)
        values_ref[at, :] = found
        for part in range(4):
            values_t_ref[(base + start) // 128 + part] = found[part * 128 : part * 128 + 128, :].T


def block_rows(ref, indices, cols):
    return jnp.concatenate(
        [ref[pl.ds(pl.multiple_of(index * 128, 128), 128), cols] for index in indices], axis=0
    )


def block_cols(ref, indices, cols):
    return jnp.concatenate([ref[index, cols, :] for index in indices], axis=1)


def by_two(count, step, carried):
    carried = lax.fori_loop(0, count // 2, lambda i, c: step(2 * i, 2, c), carried)
    return lax.fori_loop(0, count % 2, lambda i, c: step(count - 1, 1, c), carried)


def attend(meta_ref, b, first, count, keys_ref, values_t_ref, query_t_ref, keep_ref, acc_ref, old):
    pairs = query_t_ref.shape[0]
    wide = query_t_ref.shape[2]

    def peak_step(slot, size, peaks):
        indices = [meta_ref[b, first + slot + j] for j in range(size)]
        tiles = [
            dot_nn(block_rows(keys_ref, indices, slice(p * PAIR, (p + 1) * PAIR)), query_t_ref[p])
            for p in range(pairs)
        ]
        out = []
        for p in range(pairs):
            for j in range(size):
                keep_ref[slot + j, p] = tiles[p][j * 128 : (j + 1) * 128]
            out.append(jnp.maximum(peaks[p], groups_of_eight(tiles[p], jnp.maximum)))
        return tuple(out)

    if old is None:
        start = (jnp.full((8, wide), -3.0e38, F32),) * pairs
    else:
        start = tuple(jnp.broadcast_to(peak, (8, wide)) for peak, _ in old)
    peaks = by_two(count, peak_step, start)
    peaks = tuple(jnp.max(peak, axis=0, keepdims=True) for peak in peaks)
    totals = []
    for p in range(pairs):
        if old is None:
            acc_ref[p] = jnp.zeros(acc_ref.shape[1:], F32)
            totals.append(jnp.zeros((1, wide), F32))
        else:
            shrink = jnp.exp(old[p][0] - peaks[p])
            acc_ref[p] = acc_ref[p] * shrink
            totals.append(old[p][1] * shrink)

    def sum_step(slot, size, sums):
        indices = [meta_ref[b, first + slot + j] for j in range(size)]
        out = []
        for p in range(pairs):
            cols = slice(p * PAIR, (p + 1) * PAIR)
            tile = jnp.concatenate([jnp.exp(keep_ref[slot + j, p] - peaks[p]) for j in range(size)], axis=0)
            out.append(sums[p] + groups_of_eight(tile, jnp.add))
            acc_ref[p] += dot_nn(block_cols(values_t_ref, indices, cols), tile.astype(BF16))
        return tuple(out)

    sums = by_two(count, sum_step, (jnp.zeros((8, wide), F32),) * pairs)
    return [
        (peaks[p], totals[p] + jnp.sum(sums[p], axis=0, keepdims=True)) for p in range(pairs)
    ]


def own_kernel(
    meta_ref,
    own_ref,
    wq_ref,
    wk_ref,
    wv_ref,
    pack_a,
    pack_b,
    keys_ref,
    values_ref,
    keys_t_ref,
    queries_ref,
    query_t_ref,
    acc_ref,
    peaks_ref,
    sums_ref,
    keep_ref,
    values_t_ref,
):
    block = 128
    pairs = queries_ref.shape[1] // PAIR
    packs = (pack_a, pack_b)
    project_keys(own_ref, joined(wk_ref, packs, 1), joined(wv_ref, packs, 2), keys_ref, values_ref, values_t_ref, 0)
    wq = joined(wq_ref, packs, 0)
    for kb in range(keys_t_ref.shape[0]):
        keys_t_ref[kb] = keys_ref[kb * block : (kb + 1) * block, :].T

    @pl.loop(0, queries_ref.shape[0] // block)
    def _(b):
        first = pl.multiple_of(meta_ref[b, BLOCK_COL] * block, block)
        query = dot_nn(own_ref[pl.ds(first, block), :], wq).astype(BF16)
        query = (query.astype(F32) * (HD ** (-0.5))).astype(BF16)
        queries_ref[pl.ds(pl.multiple_of(b * block, block), block), :] = query
        for p in range(pairs):
            query_t_ref[b, p] = both_heads_t(query[:, p * PAIR : (p + 1) * PAIR])
        found = attend(
            meta_ref,
            b,
            0,
            meta_ref[b, OWN_COL],
            keys_ref,
            values_t_ref,
            query_t_ref.at[b],
            keep_ref,
            acc_ref.at[b],
            None,
        )
        for p in range(pairs):
            at = slice(p * 2 * block, (p + 1) * 2 * block)
            peaks_ref[pl.ds(b, 1), at] = found[p][0]
            sums_ref[pl.ds(b, 1), at] = found[p][1]


def halo_kernel(
    meta_ref,
    low_ref,
    high_ref,
    wk_ref,
    wv_ref,
    pack_a,
    pack_b,
    query_t_ref,
    old_acc_ref,
    peaks_ref,
    sums_ref,
    keys_ref,
    values_ref,
    attended_ref,
    attended_t_ref,
    log_total_ref,
    keep_ref,
    values_t_ref,
    acc_ref,
):
    block = 128
    pairs = query_t_ref.shape[1]
    wk = joined(wk_ref, (pack_a, pack_b), 1)
    wv = joined(wv_ref, (pack_a, pack_b), 2)
    project_keys(low_ref, wk, wv, keys_ref, values_ref, values_t_ref, 0)
    project_keys(high_ref, wk, wv, keys_ref, values_ref, values_t_ref, low_ref.shape[0])

    @pl.loop(0, query_t_ref.shape[0])
    def _(b):
        here = pl.ds(pl.multiple_of(b * block, block), block)
        old = []
        for p in range(pairs):
            at = slice(p * 2 * block, (p + 1) * 2 * block)
            acc_ref[p] = old_acc_ref[b, p]
            old.append((peaks_ref[pl.ds(b, 1), at], sums_ref[pl.ds(b, 1), at]))
        own = meta_ref[b, OWN_COL]
        found = attend(
            meta_ref,
            b,
            own,
            meta_ref[b, COUNT_COL] - own,
            keys_ref,
            values_t_ref,
            query_t_ref.at[b],
            keep_ref,
            acc_ref,
            old,
        )
        for p in range(pairs):
            peak, total = found[p]
            log_total_ref[pl.ds(b, 1), p * 2 * block : (p + 1) * 2 * block] = peak + jnp.log(total)
            rows = own_heads(acc_ref[p] * (1.0 / total)).astype(BF16)
            attended_t_ref[b, p * PAIR : (p + 1) * PAIR, :] = rows
            attended_ref[here, p * PAIR : (p + 1) * PAIR] = rows.T


GELU_A = 0.044715
GELU_B = 0.7978845608028654


def ffn_chunks(norm_ref, grad_ref, chunks):
    def products(at):
        up, down = chunks[at]
        return dot_nn(norm_ref[...], up), dot_nt(grad_ref[...], down)

    totals = None
    coming = products(0)
    for at, (up, down) in enumerate(chunks):
        pre, grad_act = coming
        if at + 1 < len(chunks):
            coming = products(at + 1)
        square = pre * pre
        inner = jnp.tanh(pre * (GELU_B + (GELU_A * GELU_B) * square))
        gate = 0.5 + 0.5 * inner
        active = (pre * gate).astype(BF16)
        slope = gate + pre * (1.0 - inner * inner) * (0.5 * GELU_B + (1.5 * GELU_A * GELU_B) * square)
        grad_pre = (grad_act * slope).astype(BF16)
        found = dot_nn(active, down), dot_nt(grad_pre, up)
        totals = found if totals is None else (totals[0] + found[0], totals[1] + found[1])
    return totals


def ffn_kernel(
    meta_ref,
    ordered_ref,
    grad_ref,
    attended_ref,
    gain_ref,
    wo_ref,
    pack_a,
    pack_b,
    in_ref,
    out_ref,
    hidden_ref,
    grad_rows,
    norm_ref,
    total_ref,
    back_ref,
):
    block = 128
    size = attended_ref.shape[0]
    for b in range(size // block):
        first = pl.multiple_of(meta_ref[b, BLOCK_COL] * block, block)
        hidden_ref[b * block : (b + 1) * block, :] = ordered_ref[pl.ds(first, block), :].astype(F32)
        grad_rows[b * block : (b + 1) * block, :] = grad_ref[pl.ds(first, block), :]
    share = wo_ref.shape[0]
    hidden_in = hidden_ref[...] + dot_nn(attended_ref[:, :share], wo_ref[...])
    hidden_in = hidden_in + dot_nt(attended_ref[:, share:], packed((pack_a, pack_b), 3))
    hidden_ref[...] = hidden_in
    norm_ref[...] = (hidden_in * row_scale(hidden_in) * gain_ref[...]).astype(BF16)
    cuts = [slice(start, start + 512) for start in range(0, in_ref.shape[1], 512)]
    total_ref[...], back_ref[...] = ffn_chunks(
        norm_ref, grad_rows, [(in_ref[:, at], out_ref[at, :]) for at in cuts]
    )


def rest_kernel(
    meta_ref,
    hidden_ref,
    grad_rows,
    norm_ref,
    old_total_ref,
    old_back_ref,
    gain_ref,
    wo_ref,
    pack_a,
    pack_b,
    hidden_a,
    hidden_b,
    mixed_grad_ref,
    out_own_ref,
    hidden_own_ref,
    *refs,
):
    heads = len(refs) + 1
    width = norm_ref.shape[1]
    forward, backward = ffn_chunks(
        norm_ref, grad_rows, [(ref[:width, :], ref[width:, :]) for ref in (hidden_a, hidden_b)]
    )
    hidden_in = hidden_ref[...]
    result = (hidden_in + (old_total_ref[...] + forward)).astype(BF16)
    group = meta_ref[0, GROUP_COL]
    share = out_own_ref.shape[1]
    out_own_ref[...] = chunk(result, group, share)
    scale = row_scale(hidden_in)
    second_norm = hidden_in * scale
    scaled = (old_back_ref[...] + backward) * gain_ref[...]
    hidden_grad = grad_rows[...].astype(F32) + scale * (
        scaled - second_norm * jnp.mean(scaled * second_norm, axis=-1, keepdims=True)
    )
    hidden_own_ref[...] = chunk(hidden_grad, group, share)
    for k in range(1, heads):
        who = below(group, k, heads)
        refs[k - 1][:, :share] = chunk(result, who, share)
        refs[k - 1][:, share:] = chunk(hidden_grad, who, share).astype(BF16)
    narrow = hidden_grad.astype(BF16)
    half = wo_ref.shape[0]
    mixed_grad_ref[:, :half] = dot_nt(narrow, wo_ref[...]).astype(BF16)
    mixed_grad_ref[:, half:] = dot_nn(narrow, packed((pack_a, pack_b), 3)).astype(BF16)


def back_operands(queries_ref, mixed_grad_ref, attended_t_ref, grad_t_ref, deltas_ref):
    block = 128
    pairs = queries_ref.shape[1] // PAIR

    @pl.loop(0, queries_ref.shape[0] // block)
    def _(b):
        here = pl.ds(pl.multiple_of(b * block, block), block)
        for p in range(pairs):
            cols = slice(p * PAIR, (p + 1) * PAIR)
            grad_t = both_heads_t(mixed_grad_ref[here, cols])
            grad_t_ref[b, p] = grad_t
            attended = attended_t_ref[b, cols, :].astype(F32)
            product = grad_t.astype(F32) * jnp.concatenate([attended, attended], axis=1)
            deltas_ref[pl.ds(b, 1), p * 2 * block : (p + 1) * 2 * block] = jnp.sum(product, axis=0, keepdims=True)


def scores_back(
    meta_ref,
    b,
    first,
    count,
    base,
    keys_ref,
    values_ref,
    keys_t_ref,
    operands,
    grad_keys,
    grad_values,
    rows_ref,
    acc_ref,
):
    queries_ref, query_t_ref, mixed_grad_ref, grad_t_ref, deltas_ref, log_total_ref = operands
    block = 128
    pairs = queries_ref.shape[1] // PAIR
    here = pl.ds(pl.multiple_of(b * block, block), block)
    deltas = []
    logs = []
    for p in range(pairs):
        cols = slice(p * PAIR, (p + 1) * PAIR)
        wide = slice(p * 2 * block, (p + 1) * 2 * block)
        rows_ref[0, p] = both_heads(queries_ref[here, cols])
        rows_ref[1, p] = both_heads(mixed_grad_ref[here, cols])
        deltas.append(deltas_ref[pl.ds(b, 1), wide])
        logs.append(log_total_ref[pl.ds(b, 1), wide])

    def step(slot, size, carried):
        indices = [meta_ref[b, first + slot + j] for j in range(size)]
        here = [index - base for index in indices]
        cuts = [slice(p * PAIR, (p + 1) * PAIR) for p in range(pairs)]

        def products(p):
            scores = dot_nn(block_rows(keys_ref, indices, cuts[p]), query_t_ref[b, p])
            return scores, dot_nn(block_rows(values_ref, indices, cuts[p]), grad_t_ref[b, p])

        coming = products(0)
        for p, cols in enumerate(cuts):
            scores, prob_grad = coming
            if p + 1 < pairs:
                coming = products(p + 1)
            probs = jnp.exp(scores - logs[p])
            score_grad = (probs * (prob_grad - deltas[p])).astype(BF16)
            to_values = dot_nn(probs.astype(BF16), rows_ref[1, p])
            to_keys = dot_nn(score_grad, rows_ref[0, p])
            acc_ref[p] += dot_nn(block_cols(keys_t_ref, here, cols), score_grad)
            for j in range(size):
                at = pl.ds(pl.multiple_of(here[j] * block, block), block)
                grad_values[at, cols] += to_values[j * block : (j + 1) * block]
                grad_keys[at, cols] += to_keys[j * block : (j + 1) * block]
        return carried

    by_two(count, step, 0)


def clear_back(grad_keys, grad_values):
    @pl.loop(0, grad_keys.shape[0] // 128)
    def _(kb):
        at = pl.ds(pl.multiple_of(kb * 128, 128), 128)
        grad_keys[at, :] = jnp.zeros((128, grad_keys.shape[1]), F32)
        grad_values[at, :] = jnp.zeros((128, grad_keys.shape[1]), F32)


def project_back(grad_keys, grad_values, wk, wv, start, size):
    at = slice(start, start + size)
    keys_part = dot_nt(grad_keys[at, :].astype(BF16), wk)
    return keys_part + dot_nt(grad_values[at, :].astype(BF16), wv)


def side_back_kernel(
    side,
    meta_ref,
    keys_ref,
    values_ref,
    queries_ref,
    query_t_ref,
    mixed_grad_ref,
    log_total_ref,
    wk_ref,
    wv_ref,
    pack_a,
    pack_b,
    *refs,
):
    acc_ref, grad_keys, grad_values, keys_t_ref, rows_ref = refs[-5:]
    if side == 0:
        attended_t_ref, *grads, grad_t_ref, deltas_ref = refs[:-5]
        back_operands(queries_ref, mixed_grad_ref, attended_t_ref, grad_t_ref, deltas_ref)
    else:
        grad_t_ref, deltas_ref, old_acc_ref, *grads = refs[:-5]
    operands = queries_ref, query_t_ref, mixed_grad_ref, grad_t_ref, deltas_ref, log_total_ref
    base = side * keys_t_ref.shape[0]
    clear_back(grad_keys, grad_values)

    @pl.loop(0, keys_t_ref.shape[0])
    def _(kb):
        keys_t_ref[kb] = keys_ref[pl.ds(pl.multiple_of((kb + base) * 128, 128), 128), :].T

    @pl.loop(0, queries_ref.shape[0] // 128)
    def _(b):
        own, low = meta_ref[b, OWN_COL], meta_ref[b, LOW_COL]
        acc_ref[b] = jnp.zeros(acc_ref.shape[1:], F32) if side == 0 else old_acc_ref[b]
        scores_back(
            meta_ref,
            b,
            own if side == 0 else own + low,
            low if side == 0 else meta_ref[b, COUNT_COL] - own - low,
            base,
            keys_ref,
            values_ref,
            keys_t_ref,
            operands,
            grad_keys,
            grad_values,
            rows_ref,
            acc_ref.at[b],
        )

    packs = (pack_a, pack_b)
    weights = joined(wk_ref, packs, 1), joined(wv_ref, packs, 2)
    start = 0
    for ref in grads:
        for part in range(0, ref.shape[0], 512):
            ref[part : part + 512, :] = project_back(
                grad_keys, grad_values, *weights, start + part, 512
            ).astype(BF16)
        start += ref.shape[0]


def own_back_kernel(
    meta_ref,
    keys_ref,
    values_ref,
    keys_t_ref,
    queries_ref,
    query_t_ref,
    mixed_grad_ref,
    grad_t_ref,
    deltas_ref,
    log_total_ref,
    old_acc_ref,
    wq_ref,
    wk_ref,
    wv_ref,
    pack_a,
    pack_b,
    own_ref,
    grad_keys,
    grad_values,
    rows_ref,
    acc_ref,
    query_grad,
):
    operands = queries_ref, query_t_ref, mixed_grad_ref, grad_t_ref, deltas_ref, log_total_ref
    block = 128
    rows = own_ref.shape[0]
    pairs = queries_ref.shape[1] // PAIR
    blocks = queries_ref.shape[0] // block
    clear_back(grad_keys, grad_values)

    @pl.loop(0, blocks)
    def _(b):
        acc_ref[...] = old_acc_ref[b]
        scores_back(
            meta_ref,
            b,
            0,
            meta_ref[b, OWN_COL],
            0,
            keys_ref,
            values_ref,
            keys_t_ref,
            operands,
            grad_keys,
            grad_values,
            rows_ref,
            acc_ref,
        )
        for p in range(pairs):
            found = own_heads(acc_ref[p]) * (HD ** (-0.5))
            query_grad[pl.ds(pl.multiple_of(b * block, block), block), p * PAIR : (p + 1) * PAIR] = found.T.astype(BF16)

    packs = (pack_a, pack_b)
    weights = joined(wk_ref, packs, 1), joined(wv_ref, packs, 2)
    for start in range(0, rows, 512):
        own_ref[start : start + 512, :] = project_back(grad_keys, grad_values, *weights, start, 512)
    parts = dot_nt(query_grad[...], joined(wq_ref, packs, 0))
    for b in range(blocks):
        first = pl.multiple_of(meta_ref[b, BLOCK_COL] * block, block)
        own_ref[pl.ds(first, block), :] += parts[b * block : (b + 1) * block]


def term_kernel(offset, meta_ref, own_ref, low_ref, high_ref, normed_ref, term_ref, dots_ref, *send_refs):
    rows, share = term_ref.shape
    heads = len(send_refs) + 1
    group = meta_ref[0, GROUP_COL]
    dot_rows = []
    for start in range(0, rows, 128):
        at = slice(start, start + 128)
        whole = slice(offset + start, offset + start + 128)
        term = own_ref[whole, :] + low_ref[whole, :].astype(F32) + high_ref[at, :].astype(F32)
        dots = jnp.sum(term * normed_ref[whole, :].astype(F32), axis=-1, keepdims=True)
        dot_rows.append(jnp.broadcast_to(dots, (128, 128)).T[:1])
        term_ref[at, :] = chunk(term, group, share)
        for k in range(1, heads):
            send_refs[k - 1][at, :] = chunk(term, below(group, k, heads), share).astype(BF16)
    dots = jnp.concatenate(dot_rows, axis=0)
    dots_ref[...] = dots
    high = dots.astype(BF16)
    low = (dots - high.astype(F32)).astype(BF16)
    wide = min(share, 128)
    tail = jnp.concatenate(
        [half[:, start : start + wide] for half in (high, low) for start in range(0, 128, wide)], axis=0
    )
    if share > wide:
        tail = jnp.concatenate([tail] * (share // wide), axis=1)
    for ref in send_refs:
        ref[rows:, :] = tail


def dots_of(tail):
    wide = min(tail.shape[1], 128)
    count = 128 // wide
    size = tail.shape[0] // (2 * count)
    parts = [tail[i * size : (i + 1) * size, :wide].astype(F32) for i in range(2 * count)]
    sums = [parts[i] + parts[count + i] for i in range(count)]
    return sums[0] if count == 1 else jnp.concatenate(sums, axis=1)


def back_matrix(pos_ref, first, size, total):
    place = lax.broadcasted_iota(jnp.int32, (size, total), 0) + first
    return jnp.where(jnp.broadcast_to(places(pos_ref, 0, total), (size, total)) == place, 1.0, 0.0).astype(BF16)


def place_blocks(meta_ref, refs, all_ref, first_col):
    block = 128
    share = all_ref.shape[1]
    blocks = refs[0].shape[0] // block
    for k, ref in enumerate(refs):
        cols = slice(0, share) if k == 0 else slice(first_col, first_col + share)
        for b in range(blocks):
            first = pl.multiple_of(meta_ref[k * blocks + b, BLOCK_COL] * block, block)
            all_ref[pl.ds(first, block), :] = ref[b * block : (b + 1) * block, cols].astype(all_ref.dtype)


def output_kernel(meta_ref, pos_ref, ordered_ref, gain_ref, hidden_own_ref, *refs):
    out_ref, matrix_ref, base_ref, scale_ref, norm_ref, all_ref = refs[-6:]
    own_ref, *got_refs = refs[:-6]
    place_blocks(meta_ref, [own_ref, *got_refs], all_ref, 0)
    total, share = all_ref.shape
    place_blocks(meta_ref, [hidden_own_ref, *got_refs], base_ref, share)
    for first in range(0, total, 512):
        matrix = back_matrix(pos_ref, first, 512, total)
        matrix_ref[first : first + 512, :] = matrix
        out_ref[first : first + 512, :] = dot_nn(matrix, all_ref[...]).astype(BF16)
    group = meta_ref[0, GROUP_COL]
    gain = chunk(gain_ref[...], group, share)
    for start in range(0, total, 128):
        at = slice(start, start + 128)
        ordered = ordered_ref[at, :].astype(F32)
        scale = row_scale(ordered)
        scale_ref[at, :] = scale * gain
        norm_ref[at, :] = chunk(ordered, group, share) * (scale * scale)


def final_kernel(matrix_ref, base_ref, scale_ref, norm_ref, term_a, dots_a, term_b, dots_b, *refs):
    out_ref, split_ref = refs[-2:]
    total, share = out_ref.shape
    half = total // 2
    others = (len(refs) - 2) // 2
    for i, (term_ref, dots_ref) in enumerate(((term_a, dots_a), (term_b, dots_b))):
        got_refs = refs[i * others : (i + 1) * others]
        dots = dots_ref[...]
        for ref in got_refs:
            dots = dots + dots_of(ref[half:, :])
        dots = dots * (1.0 / (share * (others + 1)))
        for start in range(0, half, 128):
            at = slice(start, start + 128)
            whole = slice(i * half + start, i * half + start + 128)
            mean = column_of(dots[start // 128 : start // 128 + 1], 128)[:, :1]
            term = term_ref[at, :]
            for ref in got_refs:
                term = term + ref[at, :].astype(F32)
            value = base_ref[whole, :] + (term * scale_ref[whole, :] - norm_ref[whole, :] * mean)
            high = value.astype(BF16)
            split_ref[whole, :share] = high
            split_ref[whole, share:] = (value - high.astype(F32)).astype(BF16)
    for first in range(0, total, 512):
        found = dot_nn(matrix_ref[first : first + 512, :], split_ref[...])
        out_ref[first : first + 512, :] = found[:, :share] + found[:, share:]


def local(
    features,
    out_grad,
    bin_order,
    key_lists,
    list_counts,
    attn_gain,
    query_weight,
    key_weight,
    value_weight,
    out_weight,
    ffn_gain,
    ffn_in,
    ffn_out,
):
    rows, width = features.shape
    block_count, slots = key_lists.shape
    block = rows // block_count
    share = query_weight.shape[1]
    hidden = ffn_in.shape[1]
    region = lax.axis_index("elem")
    regions = lax.axis_size("elem")
    group = lax.axis_index("head")
    head_groups = lax.axis_size("head")
    half_count = block_count // head_groups
    mine_rows = rows // head_groups
    forward = [(i, (i + 1) % regions) for i in range(regions)]
    backward = [(target, source) for source, target in forward]
    sibling = [(i, i ^ 1) for i in range(regions)]

    def exchanged(pieces):
        return [
            lax.ppermute(piece, "head", [(i, (i + k) % head_groups) for i in range(head_groups)])
            for k, piece in enumerate(pieces, 1)
        ]

    positions = bin_order.reshape(1, rows)
    gain_one = attn_gain.reshape(1, width)
    gain_two = ffn_gain.reshape(1, width)

    normed = call(prep_kernel, shaped((rows, width), BF16), [VMEM] * 3, vmem=60)(positions, features, gain_one)
    low = lax.ppermute(normed, "elem", forward)
    high = lax.ppermute(normed, "elem", backward)
    meta = pl.pallas_call(
        functools.partial(plan_kernel, head_groups),
        out_shape=shaped((block_count, META_COLS), jnp.int32),
        in_specs=[SMEM] * 3,
        out_specs=SMEM,
    )(jnp.stack([region, jnp.int32(regions), group, group]), key_lists, list_counts)

    ordered, grad_sorted = call(
        sort_kernel, (shaped((rows, width), BF16), shaped((rows, width), BF16)), [VMEM] * 3
    )(positions, features, out_grad)

    projections = (query_weight, key_weight, value_weight)
    if head_groups == 2:

        def my_piece(weight, core, dim):
            size = weight.shape[dim] // 2
            return lax.dynamic_slice_in_dim(weight, core * size, size, dim)

        core, normed = lax.optimization_barrier((region % 2, normed))
        mix = my_piece(out_weight, core, 0).T
        pack = jnp.concatenate([*[my_piece(w, core, 1) for w in projections], mix], axis=1)
        core, pack = lax.optimization_barrier((core, pack))
        (pack_a,) = exchanged([pack])
        hidden_pack = jnp.concatenate([my_piece(ffn_in, core, 1), my_piece(ffn_out, core, 0)], axis=0)
        (hidden_a,) = exchanged([hidden_pack])
        pack_a, meta, ordered, grad_sorted, hidden_pack = lax.optimization_barrier(
            (pack_a, meta, ordered, grad_sorted, hidden_pack)
        )
        pack_b = lax.ppermute(pack_a, "elem", sibling)
    else:

        def pieces(weight, dim):
            size = weight.shape[dim] * head_groups // 4
            whole = lax.all_gather(weight, "head", axis=dim, tiled=True)
            return jnp.split(whole, (2 * size, 3 * size), axis=dim)

        split = [pieces(w, 1) for w in projections]
        mixing = pieces(out_weight, 0)
        projections = tuple(parts[0] for parts in split)
        pack_a, pack_b = (
            jnp.concatenate([*[parts[i] for parts in split], mixing[i].T], axis=1) for i in (1, 2)
        )
        out_weight = mixing[0]
        ffn_in, *up_parts = pieces(ffn_in, 1)
        ffn_out, *down_parts = pieces(ffn_out, 0)
        hidden_a, hidden_b = (jnp.concatenate(parts, axis=0) for parts in zip(up_parts, down_parts))

    heads_width = head_groups * share
    key_value = (*projections[1:], pack_a, pack_b)
    pairs = heads_width // PAIR
    pair_tile = (pairs, PAIR, 2 * block)
    keep = pltpu.VMEM((slots, pairs, block, 2 * block), F32)
    stats = shaped((half_count, 2 * heads_width), F32)
    keys, values, keys_t, queries, query_t, part_acc, part_peaks, part_sums = call(
        own_kernel,
        (
            shaped((rows, heads_width), BF16),
            shaped((rows, heads_width), BF16),
            shaped((block_count, heads_width, block), BF16),
            shaped((mine_rows, heads_width), BF16),
            shaped((half_count,) + pair_tile, BF16),
            shaped((half_count,) + pair_tile, F32),
            stats,
            stats,
        ),
        [SMEM] + [VMEM] * 6,
        scratch=(
            keep,
            pltpu.VMEM((block_count, heads_width, block), BF16),
        ),
        vmem=26,
    )(meta, normed, *projections, pack_a, pack_b)
    halo_keys, halo_values, attended, attended_t, log_total = call(
        halo_kernel,
        (
            shaped((2 * rows, heads_width), BF16),
            shaped((2 * rows, heads_width), BF16),
            shaped((mine_rows, heads_width), BF16),
            shaped((half_count, heads_width, block), BF16),
            stats,
        ),
        [SMEM] + [VMEM] * 10,
        scratch=(
            keep,
            pltpu.VMEM((2 * block_count, heads_width, block), BF16),
            pltpu.VMEM(pair_tile, F32),
        ),
        vmem=30,
    )(meta, low, high, *key_value, query_t, part_acc, part_peaks, part_sums)

    square = shaped((mine_rows, width), F32)
    narrow = shaped((mine_rows, width), BF16)
    if head_groups == 2:
        attended, hidden_a = lax.optimization_barrier((attended, hidden_a))
        hidden_b = lax.ppermute(hidden_a, "elem", sibling)
    hidden_in, grad_rows, norm_two, part_total, part_back = call(
        ffn_kernel,
        (square, narrow, narrow, square, square),
        [SMEM] + [VMEM] * 9,
    )(meta, ordered, grad_sorted, attended, gain_two, out_weight, pack_a, pack_b, ffn_in, ffn_out)
    others = head_groups - 1
    mixed_grad, out_own, hidden_own, *sends = call(
        rest_kernel,
        (
            narrow,
            shaped((mine_rows, share), BF16),
            shaped((mine_rows, share), F32),
            *[shaped((mine_rows, 2 * share), BF16)] * others,
        ),
        [SMEM] + [VMEM] * 11,
    )(
        meta,
        hidden_in,
        grad_rows,
        norm_two,
        part_total,
        part_back,
        gain_two,
        out_weight,
        pack_a,
        pack_b,
        hidden_a,
        hidden_b,
    )
    both_got = exchanged(sends)

    rows_pair = pltpu.VMEM((2, pairs, 2 * block, PAIR), BF16)
    half = rows // 2

    def side_back(side, grads, more, *extra):
        return call(
            functools.partial(side_back_kernel, side),
            (*[shaped((size, width), BF16) for size in grads], *more, shaped((half_count,) + pair_tile, F32)),
            [SMEM] + [VMEM] * (10 + len(extra)),
            scratch=(
                pltpu.VMEM((rows, heads_width), F32),
                pltpu.VMEM((rows, heads_width), F32),
                pltpu.VMEM((block_count, heads_width, block), BF16),
                rows_pair,
            ),
            vmem=24,
        )(meta, halo_keys, halo_values, queries, query_t, mixed_grad, log_total, *key_value, *extra)

    grad_low, grad_t, deltas, part_grad = side_back(
        0, (rows,), (shaped((half_count,) + pair_tile, BF16), stats), attended_t
    )
    from_right = lax.ppermute(grad_low, "elem", backward)
    grad_high_a, grad_high_b, part_grad = side_back(1, (half, half), (), grad_t, deltas, part_grad)
    from_left = [lax.ppermute(grad, "elem", forward) for grad in (grad_high_a, grad_high_b)]
    part_grad, both_got = lax.optimization_barrier((part_grad, both_got))
    grad_own = call(
        own_back_kernel,
        shaped((rows, width), F32),
        [SMEM] + [VMEM] * 15,
        scratch=(
            pltpu.VMEM((rows, heads_width), F32),
            pltpu.VMEM((rows, heads_width), F32),
            rows_pair,
            pltpu.VMEM(pair_tile, F32),
            pltpu.VMEM((mine_rows, heads_width), BF16),
        ),
        vmem=30,
    )(
        meta,
        keys,
        values,
        keys_t,
        queries,
        query_t,
        mixed_grad,
        grad_t,
        deltas,
        log_total,
        part_grad,
        *projections,
        pack_a,
        pack_b,
    )
    tail = 2 * (half // 128) * (128 // min(share, 128))
    terms, got = [], []
    for i in range(2):
        term, dots, *sends = call(
            functools.partial(term_kernel, i * half),
            (
                shaped((half, share), F32),
                shaped((half // 128, 128), F32),
                *[shaped((half + tail, share), BF16)] * others,
            ),
            [SMEM] + [VMEM] * 4,
        )(meta, grad_own, from_right, from_left[i], normed)
        terms += [term, dots]
        got += exchanged(sends)
    columns = shaped((rows, share), F32)
    output, *prepared = call(
        output_kernel,
        (shaped((rows, share), BF16), shaped((rows, rows), BF16), columns, columns, columns),
        [SMEM] + [VMEM] * (4 + head_groups),
        scratch=(pltpu.VMEM((rows, share), BF16),),
    )(meta, positions, ordered, gain_one, hidden_own, out_own, *both_got)
    input_grad = call(
        final_kernel,
        columns,
        [VMEM] * (8 + 2 * others),
        scratch=(pltpu.VMEM((rows, 2 * share), BF16),),
    )(*prepared, *terms, *got)
    return (output, input_grad)


def solution(mesh):
    in_specs = (
        P("elem", None),
        P("elem", None),
        P("elem"),
        P("elem", None),
        P("elem"),
        P(),
        P(None, "head"),
        P(None, "head"),
        P(None, "head"),
        P("head", None),
        P(),
        P(None, "head"),
        P("head", None),
    )
    out_specs = (P("elem", "head"), P("elem", "head"))
    return jax.shard_map(local, mesh=mesh, in_specs=in_specs, out_specs=out_specs, check_vma=False)
```

profile of v0, /device:TPU:0, one launch (start us, length us, event | category | flops | bytes accessed | tf_op | source)
XLA Modules:
  0.0 105.0 jit_solution(15535989165850176994)
XLA Ops:
  0.6 0.0 copy-start.9
  0.7 0.0 copy-start.6
  0.7 3.8 %shard_map.140.own_ref.normed_ref = bf16[1024,512]{1,0:T(8,128)(2,1)} custom-call(s32[1,1024]{1,0:T(1,128)} %bitcast.6, bf16[1024,512]{1,0:T(8,128)(2,1)} %rows_ref.3, f32[1,512]{1,0:T(1,128)} %bitcast.9), custom_call_target="tpu_custom_call" | custom-call | flops 1000 | bytes 1000 | tf_op jit(solution)/shard_map/pallas_call | solution.py:820
  4.5 5.4 %collective-permute-start.2 = (bf16[1024,512]{1,0:T(8,128)(2,1)}, bf16[1024,512]{1,0:T(8,128)(2,1)}, u32[]{:S(2)}, u32[]{:S(2)}) collective-permute-start(bf16[1024,512]{1,0:T(8,128)(2,1)} %shard_map.140.own_ref.normed_ref), channel_id=1, source_target_pairs={{2,0},{4,2},{6,4},{8,6},{10,8},{12,10},{14,12},{16,14},{18,16},{20... | collective-permute-start | bytes 3145736 | tf_op jit(solution)/shard_map/ppermute | solution.py:822
  9.9 0.0 collective-permute-start.1
  9.9 0.1 copy.16
  10.1 0.9 pad_maximum_fusion.1
  11.0 1.5 %collective-permute-start = (bf16[512,512]{1,0:T(8,128)(2,1)}, bf16[512,512]{1,0:T(8,128)(2,1)S(1)}, u32[]{:S(2)}, u32[]{:S(2)}) collective-permute-start(bf16[512,512]{1,0:T(8,128)(2,1)} %pad_maximum_fusion.1), channel_id=1, source_target_pairs={{0,1},{1,0},{2,3},{3,2},{4,5},{5,4},{6,7},{7,6},{8,9},{9,8},{10,11... | collective-permute-start | bytes 1572872 | tf_op jit(solution)/shard_map/ppermute | solution.py:812
  12.7 1.1 %pad_maximum_fusion = bf16[1024,512]{1,0:T(8,128)(2,1)} fusion(bf16[512,512]{1,0:T(8,128)(2,1)S(1)} %constant_dynamic-slice_fusion, bf16[512,512]{1,0:T(8,128)(2,1)S(1)} %constant_dynamic-slice_fusion.1), kind=kLoop, calls=%fused_computation | loop fusion | flops 2097152 | bytes 2097152 | tf_op jit(solution)/shard_map/concatenate | solution.py:846
  13.7 0.5 collective-permute-start.4
  14.2 0.2 copy-done.14
  14.4 2.4 %shard_map.142 = (bf16[1024,512]{1,0:T(8,128)(2,1)S(1)}, bf16[1024,512]{1,0:T(8,128)(2,1)S(1)}) custom-call(s32[1,1024]{1,0:T(1,128)S(1)} %bitcast.7, bf16[1024,512]{1,0:T(8,128)(2,1)S(1)} %copy-done.3, bf16[1024,512]{1,0:T(8,128)(2,1)S(1)} %copy-done.14), custom_call_target="tpu_custom_call" | custom-call | flops 1000 | bytes 1000 | tf_op jit(solution)/shard_map/pallas_call | solution.py:830
  16.8 0.0 copy-start.12
  16.8 1.0 copy-done.12
  17.8 0.6 pad_add_fusion.where_ref
  18.4 3.4 %shard_map.141.meta_ref = s32[8,128]{1,0:T(8,128)} custom-call(s32[4]{0:T(128)} %pad_add_fusion.where_ref, s32[8,12]{1,0:T(8,128)} %lists_ref.1, s32[8]{0:T(128)} %counts_ref.1), custom_call_target="tpu_custom_call" | custom-call | tf_op jit(solution)/shard_map/pallas_call | solution.py:823
  21.8 4.3 %collective-permute-done.pack_a = bf16[512,512]{1,0:T(8,128)(2,1)S(1)} collective-permute-done((bf16[512,512]{1,0:T(8,128)(2,1)}, bf16[512,512]{1,0:T(8,128)(2,1)S(1)}, u32[]{:S(2)}, u32[]{:S(2)}) %collective-permute-start) | collective-permute-done | bytes 524320 | tf_op jit(solution)/shard_map/ppermute | solution.py:812
  26.1 0.0 collective-permute-start.3
  26.1 1.9 %collective-permute-done.3.pack_b = bf16[512,512]{1,0:T(8,128)(2,1)S(1)} collective-permute-done((bf16[512,512]{1,0:T(8,128)(2,1)S(1)}, bf16[512,512]{1,0:T(8,128)(2,1)S(1)}, u32[]{:S(2)}, u32[]{:S(2)}) %collective-permute-start.3) | collective-permute-done | bytes 524320 | tf_op jit(solution)/shard_map/ppermute | solution.py:851
  28.0 0.9 copy-done.10
  28.9 0.7 copy-done.15
  29.6 8.1 %shard_map.143 = (bf16[1024,512]{1,0:T(8,128)(2,1)S(1)}, bf16[1024,512]{1,0:T(8,128)(2,1)S(1)}, bf16[8,512,128]{2,1,0:T(8,128)(2,1)S(1)}, bf16[512,512]{1,0:T(8,...) custom-call(s32[8,128]{1,0:T(8,128)S(1)} %copy-done.15, ...), custom_call_target="tpu_custom_call" | custom-call | flops 1000 | bytes 1000 | tf_op jit(solution)/shard_map/pallas_call | solution.py:876
  37.8 0.0 collective-permute-done.1.low_ref
  37.8 0.0 copy-start.5
  37.8 0.0 copy-start.7
  37.8 0.0 copy-start.13
  37.8 0.0 copy-start.18
  37.8 10.7 %shard_map.144 = (bf16[2048,512]{1,0:T(8,128)(2,1)S(1)}, bf16[2048,512]{1,0:T(8,128)(2,1)S(1)}, bf16[512,512]{1,0:T(8,128)(2,1)S(1)}, bf16[4,512,128]{2,1,0:T(8,128)(2,1)S(1)}, f32[4,1024]{1,0:T(4,128)S(1)}) custom-call(s32[8,128]{1,0:T(8,128)S(1)} %copy-done.15, bf16[1024,512]{1,0:T(8,128)(2,1)} %collective-permute-done.1.low_ref, ...), custom_call_target="tpu_custom_call" | custom-call | flops 1000 | bytes 1000 | tf_op jit(solution)/shard_map/pallas_call | solution.py:895
  48.6 0.0 collective-permute-done.4.hidden_a
  48.6 0.1 collective-permute-start.5
  48.7 3.7 %shard_map.145 = (f32[512,512]{1,0:T(8,128)S(1)}, bf16[512,512]{1,0:T(8,128)(2,1)S(1)}, bf16[512,512]{1,0:T(8,128)(2,1)S(1)}, f32[512,512]{1,0:T(8,128)S(1)}, f32[512,512]{1,0:T(8,128)S(1)}) custom-call(s32[8,128]{1,0:T(8,128)S(1)} %copy-done.15, bf16[1024,512]{1,0:T(8,128)(2,1)S(1)} %get-tuple-element.62.ordered_ref, bf16[1024,512]{1,0:T(8,128)(2,1)S(1)} %copy-done.13, ...), custom_call_target="tpu_custom_call" | custom-call | flops 1000 | bytes 1000 | tf_op jit(solution)/shard_map/pallas_call | solution.py:918
  52.4 4.5 %shard_map.146 = (bf16[512,512]{1,0:T(8,128)(2,1)S(1)}, bf16[512,256]{1,0:T(8,128)(2,1)S(1)}, f32[512,256]{1,0:T(8,128)S(1)}, bf16[512,512]{1,0:T(8,128)(2,1)S(1)}) custom-call(s32[8,128]{1,0:T(8,128)S(1)} %copy-done.15, f32[512,512]{1,0:T(8,128)S(1)} %get-tuple-element.72.hidden_ref, bf16[512,512]{1,0:T(8,128)(2,1)S(1)} %get-tuple-element.73.grad_rows, ...), custom_call_target="tpu_custom_call" | custom-call | flops 1000 | bytes 1000 | tf_op jit(solution)/shard_map/pallas_call | solution.py:924
  56.9 8.6 %shard_map.147 = (bf16[1024,512]{1,0:T(8,128)(2,1)S(1)}, bf16[4,4,128,256]{3,2,1,0:T(8,128)(2,1)S(1)}, f32[4,1024]{1,0:T(4,128)S(1)}, f32[4,4,128,256]{3,2,1,0:T(8,128)S(1)}) custom-call(s32[8,128]{1,0:T(8,128)S(1)} %copy-done.15, bf16[2048,512]{1,0:T(8,128)(2,1)S(1)} %get-tuple-element.80.keys_ref, bf16[2048,512]{1,0:T(8,128)(2,1)S(1)} %get-tuple-element.81.values_ref, ...), custom_call_target="tpu_custom_call" | custom-call | flops 1000 | bytes 1000 | tf_op jit(solution)/shard_map/pallas_call | solution.py:953
  65.5 3.2 %collective-permute-start.7 = (bf16[1024,512]{1,0:T(8,128)(2,1)S(1)}, bf16[1024,512]{1,0:T(8,128)(2,1)S(1)}, u32[]{:S(2)}, u32[]{:S(2)}) collective-permute-start(bf16[1024,512]{1,0:T(8,128)(2,1)S(1)} %get-tuple-element.101), channel_id=1, source_target_pairs={{2,0},{4,2},{6,4},{8,6},{10,8},{12,10},{14,12},{16,14},{18,16},{20... | collective-permute-start | bytes 3145736 | tf_op jit(solution)/shard_map/ppermute | solution.py:969
  68.8 0.3 collective-permute-start.6
  69.1 6.4 %shard_map.148 = (bf16[512,512]{1,0:T(8,128)(2,1)S(1)}, bf16[512,512]{1,0:T(8,128)(2,1)S(1)}, f32[4,4,128,256]{3,2,1,0:T(8,128)S(1)}) custom-call(s32[8,128]{1,0:T(8,128)S(1)} %copy-done.15, bf16[2048,512]{1,0:T(8,128)(2,1)S(1)} %get-tuple-element.80.keys_ref, bf16[2048,512]{1,0:T(8,128)(2,1)S(1)} %get-tuple-element.81.values_ref, ...), custom_call_target="tpu_custom_call" | custom-call | flops 1000 | bytes 1000 | tf_op jit(solution)/shard_map/pallas_call | solution.py:953
  75.5 0.1 collective-permute-start.9
  75.5 1.8 %collective-permute-start.8 = (bf16[512,512]{1,0:T(8,128)(2,1)S(1)}, bf16[512,512]{1,0:T(8,128)(2,1)S(1)}, u32[]{:S(2)}, u32[]{:S(2)}) collective-permute-start(bf16[512,512]{1,0:T(8,128)(2,1)S(1)} %get-tuple-element.102), channel_id=1, source_target_pairs={{0,2},{2,4},{4,6},{6,8},{8,10},{10,12},{12,14},{14,16},{16,18},{18... | collective-permute-start | bytes 1572872 | tf_op jit(solution)/shard_map/ppermute | solution.py:971
  77.3 2.6 %collective-permute-done.6.refs_1_ = bf16[512,512]{1,0:T(8,128)(2,1)S(1)} collective-permute-done((bf16[512,512]{1,0:T(8,128)(2,1)S(1)}, bf16[512,512]{1,0:T(8,128)(2,1)S(1)}, u32[]{:S(2)}, u32[]{:S(2)}) %collective-permute-start.6) | collective-permute-done | bytes 524320 | tf_op jit(solution)/shard_map/ppermute | solution.py:812
  79.9 9.2 %shard_map.150.own_ref = f32[1024,512]{1,0:T(8,128)S(1)} custom-call(s32[8,128]{1,0:T(8,128)S(1)} %copy-done.15, bf16[1024,512]{1,0:T(8,128)(2,1)S(1)} %get-tuple-element.97.keys_ref, bf16[1024,512]{1,0:T(8,128)(2,1)S(1)} %get-tuple-element.98.values_ref, bf16[8,512,128]{2,1,0:T(8,128)(2,1)S(1)} %get-tuple-element.99.keys_t_ref, ...), custom_call_target="tpu_custom_call" | custom-call | flops 1000 | bytes 1000 | tf_op jit(solution)/shard_map/pallas_call | solution.py:973
  89.1 0.0 collective-permute-done.9.high_ref
  89.2 1.0 shard_map.152
  90.2 2.4 %collective-permute-start.11 = (bf16[520,256]{1,0:T(8,128)(2,1)S(1)}, bf16[520,256]{1,0:T(8,128)(2,1)S(1)}, u32[]{:S(2)}, u32[]{:S(2)}) collective-permute-start(bf16[520,256]{1,0:T(8,128)(2,1)S(1)} %get-tuple-element.109), channel_id=1, source_target_pairs={{0,1},{1,0},{2,3},{3,2},{4,5},{5,4},{6,7},{7,6},{8,9},{9,8},{10,11... | collective-permute-start | bytes 798728 | tf_op jit(solution)/shard_map/ppermute | solution.py:812
  92.6 1.0 shard_map.151
  93.6 4.6 %collective-permute-start.10 = (bf16[520,256]{1,0:T(8,128)(2,1)S(1)}, bf16[520,256]{1,0:T(8,128)(2,1)S(1)}, u32[]{:S(2)}, u32[]{:S(2)}) collective-permute-start(bf16[520,256]{1,0:T(8,128)(2,1)S(1)} %get-tuple-element.108), channel_id=1, source_target_pairs={{0,1},{1,0},{2,3},{3,2},{4,5},{5,4},{6,7},{7,6},{8,9},{9,8},{10,11... | collective-permute-start | bytes 798728 | tf_op jit(solution)/shard_map/ppermute | solution.py:812
  98.2 2.6 %shard_map.149 = (bf16[1024,256]{1,0:T(8,128)(2,1)}, bf16[1024,1024]{1,0:T(8,128)(2,1)S(1)}, f32[1024,256]{1,0:T(8,128)S(1)}, f32[1024,256]{1,0:T(8,128)S(1)}, f32[1024,256]{1,0:T(8,128)S(1)}) custom-call(s32[8,128]{1,0:T(8,128)S(1)} %copy-done.15, s32[1,1024]{1,0:T(1,128)S(1)} %bitcast.8, bf16[1024,512]{1,0:T(8,128)(2,1)S(1)} %get-tuple-element.62.ordered_ref, ...), custom_call_target="tpu_custom_call" | custom-call | flops 1000 | bytes 1000 | tf_op jit(solution)/shard_map/pallas_call | solution.py:1016
  100.8 1.8 %collective-permute-done.10.refs_0_ = bf16[520,256]{1,0:T(8,128)(2,1)S(1)} collective-permute-done((bf16[520,256]{1,0:T(8,128)(2,1)S(1)}, bf16[520,256]{1,0:T(8,128)(2,1)S(1)}, u32[]{:S(2)}, u32[]{:S(2)}) %collective-permute-start.10) | collective-permute-done | bytes 266272 | tf_op jit(solution)/shard_map/ppermute | solution.py:812
  102.6 2.4 %shard_map.153 = f32[1024,256]{1,0:T(8,128)} custom-call(bf16[1024,1024]{1,0:T(8,128)(2,1)S(1)} %get-tuple-element.93.matrix_ref, f32[1024,256]{1,0:T(8,128)S(1)} %get-tuple-element.94.base_ref, f32[1024,256]{1,0:T(8,128)S(1)} %get-tuple-element.95.scale_ref, f32[1024,256]{1,0:T(8,128)S(1)} %get-tuple-element.96.norm_ref, ...), custom_call_target="tpu_custom_call" | custom-call | flops 1000 | bytes 1000 | tf_op jit(solution)/shard_map/pallas_call | solution.py:1022
  (37 shorter events, 0.2 us)
Async XLA Ops:
  0.6 9.3 %copy-start.8 = (bf16[256,512]{1,0:T(8,128)(2,1)S(1)}, bf16[256,512]{1,0:T(8,128)(2,1)}, u32[]{:S(2)}) copy-start(bf16[256,512]{1,0:T(8,128)(2,1)} %wo_ref.3) | copy-start | bytes 786436
  0.6 9.4 %copy-start.9 = (bf16[512,256]{1,0:T(8,128)(2,1)S(1)}, bf16[512,256]{1,0:T(8,128)(2,1)}, u32[]{:S(2)}) copy-start(bf16[512,256]{1,0:T(8,128)(2,1)} %wq_ref.3) | copy-start | bytes 786436
  0.7 9.4 %copy-start.2 = (bf16[512,256]{1,0:T(8,128)(2,1)S(1)}, bf16[512,256]{1,0:T(8,128)(2,1)}, u32[]{:S(2)}) copy-start(bf16[512,256]{1,0:T(8,128)(2,1)} %wv_ref.9) | copy-start | bytes 786436
  0.7 9.4 %copy-start.1 = (bf16[512,256]{1,0:T(8,128)(2,1)S(1)}, bf16[512,256]{1,0:T(8,128)(2,1)}, u32[]{:S(2)}) copy-start(bf16[512,256]{1,0:T(8,128)(2,1)} %wk_ref.9) | copy-start | bytes 786436
  0.7 11.9 %copy-start.6 = (bf16[1024,512]{1,0:T(8,128)(2,1)S(1)}, bf16[1024,512]{1,0:T(8,128)(2,1)}, u32[]{:S(2)}) copy-start(bf16[1024,512]{1,0:T(8,128)(2,1)} %out_ref.1) | copy-start | bytes 3145732
  4.5 8.1 %copy-start.4 = (bf16[512,1024]{1,0:T(8,128)(2,1)S(1)}, bf16[512,1024]{1,0:T(8,128)(2,1)}, u32[]{:S(2)}) copy-start(bf16[512,1024]{1,0:T(8,128)(2,1)} %in_ref.1) | copy-start | bytes 3145732
  4.5 33.3 %collective-permute-start.2 = (bf16[1024,512]{1,0:T(8,128)(2,1)}, bf16[1024,512]{1,0:T(8,128)(2,1)}, u32[]{:S(2)}, u32[]{:S(2)}) collective-permute-start(bf16[1024,512]{1,0:T(8,128)(2,1)} %shard_map.140.own_ref.normed_ref), channel_id=1, source_target_pairs={{2,0},{4,2},{6,4},{8,6},{10,8},{12,10},{14,12},{16,14},{18,16},{20... | collective-permute-start | bytes 3145736 | tf_op jit(solution)/shard_map/ppermute | solution.py:822
  9.9 27.9 %collective-permute-start.1 = (bf16[1024,512]{1,0:T(8,128)(2,1)}, bf16[1024,512]{1,0:T(8,128)(2,1)}, u32[]{:S(2)}, u32[]{:S(2)}) collective-permute-start(bf16[1024,512]{1,0:T(8,128)(2,1)} %shard_map.140.own_ref.normed_ref), channel_id=1, source_target_pairs={{0,2},{2,4},{4,6},{6,8},{8,10},{10,12},{12,14},{14,16},{16,18},{18... | collective-permute-start | bytes 3145736 | tf_op jit(solution)/shard_map/ppermute | solution.py:821
  11.0 15.1 %collective-permute-start = (bf16[512,512]{1,0:T(8,128)(2,1)}, bf16[512,512]{1,0:T(8,128)(2,1)S(1)}, u32[]{:S(2)}, u32[]{:S(2)}) collective-permute-start(bf16[512,512]{1,0:T(8,128)(2,1)} %pad_maximum_fusion.1), channel_id=1, source_target_pairs={{0,1},{1,0},{2,3},{3,2},{4,5},{5,4},{6,7},{7,6},{8,9},{9,8},{10,11... | collective-permute-start | bytes 1572872 | tf_op jit(solution)/shard_map/ppermute | solution.py:812
  12.5 1.7 %copy-start.3 = (bf16[1024,512]{1,0:T(8,128)(2,1)S(1)}, bf16[1024,512]{1,0:T(8,128)(2,1)}, u32[]{:S(2)}) copy-start(bf16[1024,512]{1,0:T(8,128)(2,1)} %rows_ref.3) | copy-start | bytes 3145732
  12.5 1.9 %copy-start.14 = (bf16[1024,512]{1,0:T(8,128)(2,1)S(1)}, bf16[1024,512]{1,0:T(8,128)(2,1)}, u32[]{:S(2)}) copy-start(bf16[1024,512]{1,0:T(8,128)(2,1)} %grads_ref.1) | copy-start | bytes 3145732
  12.5 1.9 %copy-start.16 = (s32[1024]{0:T(1024)S(1)}, s32[1024]{0:T(1024)}, u32[]{:S(2)}) copy-start(s32[1024]{0:T(1024)} %param.15) | copy-start | bytes 12292
  12.6 15.3 %copy-start = (bf16[1024,512]{1,0:T(8,128)(2,1)S(1)}, bf16[1024,512]{1,0:T(8,128)(2,1)}, u32[]{:S(2)}) copy-start(bf16[1024,512]{1,0:T(8,128)(2,1)} %shard_map.140.own_ref.normed_ref) | copy-start | bytes 3145732
  13.7 34.8 %collective-permute-start.4 = (bf16[1024,512]{1,0:T(8,128)(2,1)}, bf16[1024,512]{1,0:T(8,128)(2,1)}, u32[]{:S(2)}, u32[]{:S(2)}) collective-permute-start(bf16[1024,512]{1,0:T(8,128)(2,1)} %pad_maximum_fusion), channel_id=1, source_target_pairs={{0,1},{1,0},{2,3},{3,2},{4,5},{5,4},{6,7},{7,6},{8,9},{9,8},{10,11... | collective-permute-start | bytes 3145736 | tf_op jit(solution)/shard_map/ppermute | solution.py:812
  16.8 1.0 copy-start.12
  26.1 1.9 %collective-permute-start.3 = (bf16[512,512]{1,0:T(8,128)(2,1)S(1)}, bf16[512,512]{1,0:T(8,128)(2,1)S(1)}, u32[]{:S(2)}, u32[]{:S(2)}) collective-permute-start(bf16[512,512]{1,0:T(8,128)(2,1)S(1)} %collective-permute-done.pack_a), channel_id=1, source_target_pairs={{0,2},{2,0},{4,6},{6,4},{8,10},{10,8},{12,14},{14,12},{16,18},{18,... | collective-permute-start | bytes 1572872 | tf_op jit(solution)/shard_map/ppermute | solution.py:851
  28.0 1.0 copy-start.10
  28.9 0.7 copy-start.15
  37.8 10.9 %copy-start.5 = (bf16[512,1024]{1,0:T(8,128)(2,1)S(1)}, bf16[512,1024]{1,0:T(8,128)(2,1)}, u32[]{:S(2)}) copy-start(bf16[512,1024]{1,0:T(8,128)(2,1)} %in_ref.1) | copy-start | bytes 3145732
  37.8 10.9 %copy-start.7 = (bf16[1024,512]{1,0:T(8,128)(2,1)S(1)}, bf16[1024,512]{1,0:T(8,128)(2,1)}, u32[]{:S(2)}) copy-start(bf16[1024,512]{1,0:T(8,128)(2,1)} %out_ref.1) | copy-start | bytes 3145732
  37.8 10.9 %copy-start.13 = (bf16[1024,512]{1,0:T(8,128)(2,1)S(1)}, bf16[1024,512]{1,0:T(8,128)(2,1)}, u32[]{:S(2)}) copy-start(bf16[1024,512]{1,0:T(8,128)(2,1)} %copy-done.12) | copy-start | bytes 3145732
  37.8 10.9 %copy-start.18 = (f32[512]{0:T(512)S(1)}, f32[512]{0:T(512)}, u32[]{:S(2)}) copy-start(f32[512]{0:T(512)} %param.23) | copy-start | bytes 6148
  48.6 3.9 %collective-permute-start.5 = (bf16[1024,512]{1,0:T(8,128)(2,1)}, bf16[1024,512]{1,0:T(8,128)(2,1)S(1)}, u32[]{:S(2)}, u32[]{:S(2)}) collective-permute-start(bf16[1024,512]{1,0:T(8,128)(2,1)} %collective-permute-done.4.hidden_a), channel_id=1, source_target_pairs={{0,2},{2,0},{4,6},{6,4},{8,10},{10,8},{12,14},{14,12},{16,18},{18,... | collective-permute-start | bytes 3145736 | tf_op jit(solution)/shard_map/ppermute | solution.py:917
  65.5 23.6 %collective-permute-start.7 = (bf16[1024,512]{1,0:T(8,128)(2,1)S(1)}, bf16[1024,512]{1,0:T(8,128)(2,1)S(1)}, u32[]{:S(2)}, u32[]{:S(2)}) collective-permute-start(bf16[1024,512]{1,0:T(8,128)(2,1)S(1)} %get-tuple-element.101), channel_id=1, source_target_pairs={{2,0},{4,2},{6,4},{8,6},{10,8},{12,10},{14,12},{16,14},{18,16},{20... | collective-permute-start | bytes 3145736 | tf_op jit(solution)/shard_map/ppermute | solution.py:969
  68.8 11.1 %collective-permute-start.6 = (bf16[512,512]{1,0:T(8,128)(2,1)S(1)}, bf16[512,512]{1,0:T(8,128)(2,1)S(1)}, u32[]{:S(2)}, u32[]{:S(2)}) collective-permute-start(bf16[512,512]{1,0:T(8,128)(2,1)S(1)} %get-tuple-element.90), channel_id=1, source_target_pairs={{0,1},{1,0},{2,3},{3,2},{4,5},{5,4},{6,7},{7,6},{8,9},{9,8},{10,11... | collective-permute-start | bytes 1572872 | tf_op jit(solution)/shard_map/ppermute | solution.py:812
  69.1 10.9 %copy-start.11 = (bf16[512,256]{1,0:T(8,128)(2,1)S(1)}, bf16[512,256]{1,0:T(8,128)(2,1)}, u32[]{:S(2)}) copy-start(bf16[512,256]{1,0:T(8,128)(2,1)} %wq_ref.3) | copy-start | bytes 786436
  75.5 13.7 %collective-permute-start.9 = (bf16[512,512]{1,0:T(8,128)(2,1)S(1)}, bf16[512,512]{1,0:T(8,128)(2,1)S(1)}, u32[]{:S(2)}, u32[]{:S(2)}) collective-permute-start(bf16[512,512]{1,0:T(8,128)(2,1)S(1)} %get-tuple-element.105), channel_id=1, source_target_pairs={{0,2},{2,4},{4,6},{6,8},{8,10},{10,12},{12,14},{14,16},{16,18},{18... | collective-permute-start | bytes 1572872 | tf_op jit(solution)/shard_map/ppermute | solution.py:971
  75.5 17.1 %collective-permute-start.8 = (bf16[512,512]{1,0:T(8,128)(2,1)S(1)}, bf16[512,512]{1,0:T(8,128)(2,1)S(1)}, u32[]{:S(2)}, u32[]{:S(2)}) collective-permute-start(bf16[512,512]{1,0:T(8,128)(2,1)S(1)} %get-tuple-element.102), channel_id=1, source_target_pairs={{0,2},{2,4},{4,6},{6,8},{8,10},{10,12},{12,14},{14,16},{16,18},{18... | collective-permute-start | bytes 1572872 | tf_op jit(solution)/shard_map/ppermute | solution.py:971
  90.2 8.0 %copy-start.17 = (f32[512]{0:T(512)S(1)}, f32[512]{0:T(512)}, u32[]{:S(2)}) copy-start(f32[512]{0:T(512)} %param.18) | copy-start | bytes 6148
  90.2 10.6 %collective-permute-start.11 = (bf16[520,256]{1,0:T(8,128)(2,1)S(1)}, bf16[520,256]{1,0:T(8,128)(2,1)S(1)}, u32[]{:S(2)}, u32[]{:S(2)}) collective-permute-start(bf16[520,256]{1,0:T(8,128)(2,1)S(1)} %get-tuple-element.109), channel_id=1, source_target_pairs={{0,1},{1,0},{2,3},{3,2},{4,5},{5,4},{6,7},{7,6},{8,9},{9,8},{10,11... | collective-permute-start | bytes 798728 | tf_op jit(solution)/shard_map/ppermute | solution.py:812
  93.6 9.0 %collective-permute-start.10 = (bf16[520,256]{1,0:T(8,128)(2,1)S(1)}, bf16[520,256]{1,0:T(8,128)(2,1)S(1)}, u32[]{:S(2)}, u32[]{:S(2)}) collective-permute-start(bf16[520,256]{1,0:T(8,128)(2,1)S(1)} %get-tuple-element.108), channel_id=1, source_target_pairs={{0,1},{1,0},{2,3},{3,2},{4,5},{5,4},{6,7},{7,6},{8,9},{9,8},{10,11... | collective-permute-start | bytes 798728 | tf_op jit(solution)/shard_map/ppermute | solution.py:812
where the time goes:
time: 104 us; the launch traced here: 105 us
  Pallas kernels  67.8 us (65%)
  starting transfers between devices  20 us (19%)
  waiting for transfers between devices  10.6 us (10%)
  local copies, waits for them, and re-layouts  3.14 us (3%)
  other arithmetic  2.55 us (2%)
    pallas_call x2, Pallas kernels, side_back(): call(functools.partial(side_back_kernel, side), (*[shaped((size, width),...  15 us
    pallas_call x1, Pallas kernels, local(): call(halo_kernel, (shaped((2 * rows, heads_width), BF16), shaped((2 * row...  10.7 us
    ppermute x5, starting transfers between devices, exchanged(): lax.ppermute(piece, 'head', [(i, (i + k) % head_groups) for i in range(he...  9.37 us
    pallas_call x1, Pallas kernels, local(): call(own_back_kernel, shaped((rows, width), F32), [SMEM] + [VMEM] * 15, s...  9.2 us
    ppermute x5, waiting for transfers between devices, exchanged(): lax.ppermute(piece, 'head', [(i, (i + k) % head_groups) for i in range(he...  8.67 us
    pallas_call x1, Pallas kernels, local(): call(own_kernel, (shaped((rows, heads_width), BF16), shaped((rows, heads_...  8.14 us
    ppermute x1, starting transfers between devices, local(): high = lax.ppermute(normed, 'elem', backward)  5.41 us
    pallas_call x1, Pallas kernels, local(): call(rest_kernel, (narrow, shaped((mine_rows, share), BF16), shaped((mine...  4.46 us
  transfers between devices with their start and end apart: 12, of which 4 were waited for; matrix products, arithmetic and copies ran while one was open for 3% of the time, Pallas kernels for 46%

commit v1 on v0

--- a/solution.py
+++ b/solution.py
@@ -550,8 +550,8 @@
 
 def project_back(grad_keys, grad_values, wk, wv, start, size):
     at = slice(start, start + size)
-    keys_part = dot_nt(grad_keys[at, :].astype(BF16), wk)
-    return keys_part + dot_nt(grad_values[at, :].astype(BF16), wv)
+    grads = jnp.concatenate([grad_keys[at, :].astype(BF16), grad_values[at, :].astype(BF16)], axis=1)
+    return dot_nt(grads, jnp.concatenate([wk, wv], axis=1))
 
 
 def side_back_kernel(

time: 104 us -> 102 us (0.981); the launches traced: 105 us -> 100 us
  Pallas kernels: 67.8 us -> 62 us
  waiting for transfers between devices: 10.6 us -> 16 us
  starting transfers between devices: 20 us -> 15.5 us
    ppermute x5, starting transfers between devices: 9.37 us -> 5.52 us  [exchanged(): lax.ppermute(piece, 'head', [(i, (i + k) % head_groups) for i in range(he...]
    ppermute x2, waiting for transfers between devices: 0.01 us -> 2.99 us  [local(): lax.ppermute(grad, 'elem', forward)]
    ppermute x5, waiting for transfers between devices: 8.67 us -> 11.1 us  [exchanged(): lax.ppermute(piece, 'head', [(i, (i + k) % head_groups) for i in range(he...]
    pallas_call x1, Pallas kernels: 10.7 us -> 8.67 us  [local(): call(halo_kernel, (shaped((2 * rows, heads_width), BF16), shaped((2 * row...]
    ppermute x2, starting transfers between devices: 1.86 us -> 0.12 us  [local(): lax.ppermute(grad, 'elem', forward)]
    pallas_call x1, Pallas kernels: 9.2 us -> 7.78 us  [local(): call(own_back_kernel, shaped((rows, width), F32), [SMEM] + [VMEM] * 15, s...]
    pallas_call x2, Pallas kernels: 15 us -> 13.8 us  [side_back(): call(functools.partial(side_back_kernel, side), (*[shaped((size, width),...]
    pallas_call x1, Pallas kernels: 8.14 us -> 7.04 us  [local(): call(own_kernel, (shaped((rows, heads_width), BF16), shaped((rows, heads_...]
  transfers between devices with their start and end apart: 12 -> 12, of which waited for: 4 -> 5; matrix products, arithmetic and copies ran while one was open for 3% -> 3% of each run, Pallas kernels for 46% -> 44%
where the time goes in v1:
time: 102 us; the launch traced here: 100 us
  Pallas kernels  62 us (61%)
  waiting for transfers between devices  16 us (16%)
  starting transfers between devices  15.5 us (15%)
  local copies, waits for them, and re-layouts  3.14 us (3%)
  other arithmetic  2.55 us (2%)
    pallas_call x2, Pallas kernels, side_back(): call(functools.partial(side_back_kernel, side), (*[shaped((size, width),...  13.8 us
    ppermute x5, waiting for transfers between devices, exchanged(): lax.ppermute(piece, 'head', [(i, (i + k) % head_groups) for i in range(he...  11.1 us
    pallas_call x1, Pallas kernels, local(): call(halo_kernel, (shaped((2 * rows, heads_width), BF16), shaped((2 * row...  8.67 us
    pallas_call x1, Pallas kernels, local(): call(own_back_kernel, shaped((rows, width), F32), [SMEM] + [VMEM] * 15, s...  7.78 us
    pallas_call x1, Pallas kernels, local(): call(own_kernel, (shaped((rows, heads_width), BF16), shaped((rows, heads_...  7.04 us
    ppermute x5, starting transfers between devices, exchanged(): lax.ppermute(piece, 'head', [(i, (i + k) % head_groups) for i in range(he...  5.52 us
    ppermute x1, starting transfers between devices, local(): high = lax.ppermute(normed, 'elem', backward)  5.41 us
    pallas_call x1, Pallas kernels, local(): call(rest_kernel, (narrow, shaped((mine_rows, share), BF16), shaped((mine...  4.46 us
  transfers between devices with their start and end apart: 12, of which 5 were waited for; matrix products, arithmetic and copies ran while one was open for 3% of the time, Pallas kernels for 44%

profile of v1, /device:TPU:0, one launch (start us, length us, event | category | flops | bytes accessed | tf_op | source)
XLA Modules:
  0.0 100.2 jit_solution(7656273051236556948)
XLA Ops:
  0.6 0.0 copy-start.9
  0.7 0.0 copy-start.6
  0.7 3.8 %shard_map.140.own_ref.normed_ref = bf16[1024,512]{1,0:T(8,128)(2,1)} custom-call(s32[1,1024]{1,0:T(1,128)} %bitcast.6, bf16[1024,512]{1,0:T(8,128)(2,1)} %rows_ref.3, f32[1,512]{1,0:T(1,128)} %bitcast.9), custom_call_target="tpu_custom_call" | custom-call | flops 1000 | bytes 1000 | tf_op jit(solution)/shard_map/pallas_call | solution.py:820
  4.5 5.4 %collective-permute-start.2 = (bf16[1024,512]{1,0:T(8,128)(2,1)}, bf16[1024,512]{1,0:T(8,128)(2,1)}, u32[]{:S(2)}, u32[]{:S(2)}) collective-permute-start(bf16[1024,512]{1,0:T(8,128)(2,1)} %shard_map.140.own_ref.normed_ref), channel_id=1, source_target_pairs={{2,0},{4,2},{6,4},{8,6},{10,8},{12,10},{14,12},{16,14},{18,16},{20... | collective-permute-start | bytes 3145736 | tf_op jit(solution)/shard_map/ppermute | solution.py:822
  9.9 0.1 copy.16
  10.1 0.9 pad_maximum_fusion.1
  11.0 1.5 %collective-permute-start = (bf16[512,512]{1,0:T(8,128)(2,1)}, bf16[512,512]{1,0:T(8,128)(2,1)S(1)}, u32[]{:S(2)}, u32[]{:S(2)}) collective-permute-start(bf16[512,512]{1,0:T(8,128)(2,1)} %pad_maximum_fusion.1), channel_id=1, source_target_pairs={{0,1},{1,0},{2,3},{3,2},{4,5},{5,4},{6,7},{7,6},{8,9},{9,8},{10,11... | collective-permute-start | bytes 1572872 | tf_op jit(solution)/shard_map/ppermute | solution.py:812
  12.7 1.1 %pad_maximum_fusion = bf16[1024,512]{1,0:T(8,128)(2,1)} fusion(bf16[512,512]{1,0:T(8,128)(2,1)S(1)} %constant_dynamic-slice_fusion, bf16[512,512]{1,0:T(8,128)(2,1)S(1)} %constant_dynamic-slice_fusion.1), kind=kLoop, calls=%fused_computation | loop fusion | flops 2097152 | bytes 2097152 | tf_op jit(solution)/shard_map/concatenate | solution.py:846
  13.7 0.5 collective-permute-start.4
  14.2 0.2 copy-done.14
  14.4 2.4 %shard_map.142 = (bf16[1024,512]{1,0:T(8,128)(2,1)S(1)}, bf16[1024,512]{1,0:T(8,128)(2,1)S(1)}) custom-call(s32[1,1024]{1,0:T(1,128)S(1)} %bitcast.7, bf16[1024,512]{1,0:T(8,128)(2,1)S(1)} %copy-done.3, bf16[1024,512]{1,0:T(8,128)(2,1)S(1)} %copy-done.14), custom_call_target="tpu_custom_call" | custom-call | flops 1000 | bytes 1000 | tf_op jit(solution)/shard_map/pallas_call | solution.py:830
  16.8 0.0 copy-start.12
  16.8 1.0 copy-done.12
  17.8 0.6 pad_add_fusion.where_ref
  18.4 3.4 %shard_map.141.meta_ref = s32[8,128]{1,0:T(8,128)} custom-call(s32[4]{0:T(128)} %pad_add_fusion.where_ref, s32[8,12]{1,0:T(8,128)} %lists_ref.1, s32[8]{0:T(128)} %counts_ref.1), custom_call_target="tpu_custom_call" | custom-call | tf_op jit(solution)/shard_map/pallas_call | solution.py:823
  21.8 4.3 %collective-permute-done.pack_a = bf16[512,512]{1,0:T(8,128)(2,1)S(1)} collective-permute-done((bf16[512,512]{1,0:T(8,128)(2,1)}, bf16[512,512]{1,0:T(8,128)(2,1)S(1)}, u32[]{:S(2)}, u32[]{:S(2)}) %collective-permute-start) | collective-permute-done | bytes 524320 | tf_op jit(solution)/shard_map/ppermute | solution.py:812
  26.1 0.0 collective-permute-start.3
  26.1 1.9 %collective-permute-done.3.pack_b = bf16[512,512]{1,0:T(8,128)(2,1)S(1)} collective-permute-done((bf16[512,512]{1,0:T(8,128)(2,1)S(1)}, bf16[512,512]{1,0:T(8,128)(2,1)S(1)}, u32[]{:S(2)}, u32[]{:S(2)}) %collective-permute-start.3) | collective-permute-done | bytes 524320 | tf_op jit(solution)/shard_map/ppermute | solution.py:851
  28.0 0.9 copy-done.10
  28.9 0.7 copy-done.15
  29.6 7.0 %shard_map.143 = (bf16[1024,512]{1,0:T(8,128)(2,1)S(1)}, bf16[1024,512]{1,0:T(8,128)(2,1)S(1)}, bf16[8,512,128]{2,1,0:T(8,128)(2,1)S(1)}, bf16[512,512]{1,0:T(8,...) custom-call(s32[8,128]{1,0:T(8,128)S(1)} %copy-done.15, ...), custom_call_target="tpu_custom_call" | custom-call | flops 1000 | bytes 1000 | tf_op jit(solution)/shard_map/pallas_call | solution.py:876
  36.7 0.0 collective-permute-done.1.low_ref
  36.7 0.0 copy-start.5
  36.7 0.0 copy-start.7
  36.7 0.0 copy-start.13
  36.7 0.0 copy-start.18
  36.7 8.7 %shard_map.144 = (bf16[2048,512]{1,0:T(8,128)(2,1)S(1)}, bf16[2048,512]{1,0:T(8,128)(2,1)S(1)}, bf16[512,512]{1,0:T(8,128)(2,1)S(1)}, bf16[4,512,128]{2,1,0:T(8,128)(2,1)S(1)}, f32[4,1024]{1,0:T(4,128)S(1)}) custom-call(s32[8,128]{1,0:T(8,128)S(1)} %copy-done.15, bf16[1024,512]{1,0:T(8,128)(2,1)} %collective-permute-done.1.low_ref, ...), custom_call_target="tpu_custom_call" | custom-call | flops 1000 | bytes 1000 | tf_op jit(solution)/shard_map/pallas_call | solution.py:895
  45.4 0.0 collective-permute-done.4.hidden_a
  45.4 1.0 %collective-permute-start.5 = (bf16[1024,512]{1,0:T(8,128)(2,1)}, bf16[1024,512]{1,0:T(8,128)(2,1)S(1)}, u32[]{:S(2)}, u32[]{:S(2)}) collective-permute-start(bf16[1024,512]{1,0:T(8,128)(2,1)} %collective-permute-done.4.hidden_a), channel_id=1, source_target_pairs={{0,2},{2,0},{4,6},{6,4},{8,10},{10,8},{12,14},{14,12},{16,18},{18,... | collective-permute-start | bytes 3145736 | tf_op jit(solution)/shard_map/ppermute | solution.py:917
  46.4 3.7 %shard_map.145 = (f32[512,512]{1,0:T(8,128)S(1)}, bf16[512,512]{1,0:T(8,128)(2,1)S(1)}, bf16[512,512]{1,0:T(8,128)(2,1)S(1)}, f32[512,512]{1,0:T(8,128)S(1)}, f32[512,512]{1,0:T(8,128)S(1)}) custom-call(s32[8,128]{1,0:T(8,128)S(1)} %copy-done.15, bf16[1024,512]{1,0:T(8,128)(2,1)S(1)} %get-tuple-element.62.ordered_ref, bf16[1024,512]{1,0:T(8,128)(2,1)S(1)} %copy-done.13, ...), custom_call_target="tpu_custom_call" | custom-call | flops 1000 | bytes 1000 | tf_op jit(solution)/shard_map/pallas_call | solution.py:918
  50.2 4.5 %shard_map.146 = (bf16[512,512]{1,0:T(8,128)(2,1)S(1)}, bf16[512,256]{1,0:T(8,128)(2,1)S(1)}, f32[512,256]{1,0:T(8,128)S(1)}, bf16[512,512]{1,0:T(8,128)(2,1)S(1)}) custom-call(s32[8,128]{1,0:T(8,128)S(1)} %copy-done.15, f32[512,512]{1,0:T(8,128)S(1)} %get-tuple-element.72.hidden_ref, bf16[512,512]{1,0:T(8,128)(2,1)S(1)} %get-tuple-element.73.grad_rows, ...), custom_call_target="tpu_custom_call" | custom-call | flops 1000 | bytes 1000 | tf_op jit(solution)/shard_map/pallas_call | solution.py:924
  54.7 7.7 %shard_map.147 = (bf16[1024,512]{1,0:T(8,128)(2,1)S(1)}, bf16[4,4,128,256]{3,2,1,0:T(8,128)(2,1)S(1)}, f32[4,1024]{1,0:T(4,128)S(1)}, f32[4,4,128,256]{3,2,1,0:T(8,128)S(1)}) custom-call(s32[8,128]{1,0:T(8,128)S(1)} %copy-done.15, bf16[2048,512]{1,0:T(8,128)(2,1)S(1)} %get-tuple-element.80.keys_ref, bf16[2048,512]{1,0:T(8,128)(2,1)S(1)} %get-tuple-element.81.values_ref, ...), custom_call_target="tpu_custom_call" | custom-call | flops 1000 | bytes 1000 | tf_op jit(solution)/shard_map/pallas_call | solution.py:953
  62.4 3.5 %collective-permute-start.7 = (bf16[1024,512]{1,0:T(8,128)(2,1)S(1)}, bf16[1024,512]{1,0:T(8,128)(2,1)S(1)}, u32[]{:S(2)}, u32[]{:S(2)}) collective-permute-start(bf16[1024,512]{1,0:T(8,128)(2,1)S(1)} %get-tuple-element.101), channel_id=1, source_target_pairs={{2,0},{4,2},{6,4},{8,6},{10,8},{12,10},{14,12},{16,14},{18,16},{20... | collective-permute-start | bytes 3145736 | tf_op jit(solution)/shard_map/ppermute | solution.py:969
  65.8 0.8 collective-permute-start.6
  66.6 6.1 %shard_map.148 = (bf16[512,512]{1,0:T(8,128)(2,1)S(1)}, bf16[512,512]{1,0:T(8,128)(2,1)S(1)}, f32[4,4,128,256]{3,2,1,0:T(8,128)S(1)}) custom-call(s32[8,128]{1,0:T(8,128)S(1)} %copy-done.15, bf16[2048,512]{1,0:T(8,128)(2,1)S(1)} %get-tuple-element.80.keys_ref, bf16[2048,512]{1,0:T(8,128)(2,1)S(1)} %get-tuple-element.81.values_ref, ...), custom_call_target="tpu_custom_call" | custom-call | flops 1000 | bytes 1000 | tf_op jit(solution)/shard_map/pallas_call | solution.py:953
  72.7 0.1 collective-permute-start.9
  72.8 0.1 collective-permute-start.8
  72.8 3.9 %collective-permute-done.6.refs_1_ = bf16[512,512]{1,0:T(8,128)(2,1)S(1)} collective-permute-done((bf16[512,512]{1,0:T(8,128)(2,1)S(1)}, bf16[512,512]{1,0:T(8,128)(2,1)S(1)}, u32[]{:S(2)}, u32[]{:S(2)}) %collective-permute-start.6) | collective-permute-done | bytes 524320 | tf_op jit(solution)/shard_map/ppermute | solution.py:812
  76.8 7.8 %shard_map.150.own_ref = f32[1024,512]{1,0:T(8,128)S(1)} custom-call(s32[8,128]{1,0:T(8,128)S(1)} %copy-done.15, bf16[1024,512]{1,0:T(8,128)(2,1)S(1)} %get-tuple-element.97.keys_ref, bf16[1024,512]{1,0:T(8,128)(2,1)S(1)} %get-tuple-element.98.values_ref, bf16[8,512,128]{2,1,0:T(8,128)(2,1)S(1)} %get-tuple-element.99.keys_t_ref, ...), custom_call_target="tpu_custom_call" | custom-call | flops 1000 | bytes 1000 | tf_op jit(solution)/shard_map/pallas_call | solution.py:973
  84.6 0.0 collective-permute-done.9.high_ref
  84.6 1.0 shard_map.152
  85.6 1.1 %collective-permute-start.11 = (bf16[520,256]{1,0:T(8,128)(2,1)S(1)}, bf16[520,256]{1,0:T(8,128)(2,1)S(1)}, u32[]{:S(2)}, u32[]{:S(2)}) collective-permute-start(bf16[520,256]{1,0:T(8,128)(2,1)S(1)} %get-tuple-element.109), channel_id=1, source_target_pairs={{0,1},{1,0},{2,3},{3,2},{4,5},{5,4},{6,7},{7,6},{8,9},{9,8},{10,11... | collective-permute-start | bytes 798728 | tf_op jit(solution)/shard_map/ppermute | solution.py:812
  86.7 3.0 %collective-permute-done.8.high_ref = bf16[512,512]{1,0:T(8,128)(2,1)S(1)} collective-permute-done((bf16[512,512]{1,0:T(8,128)(2,1)S(1)}, bf16[512,512]{1,0:T(8,128)(2,1)S(1)}, u32[]{:S(2)}, u32[]{:S(2)}) %collective-permute-start.8) | collective-permute-done | bytes 524320 | tf_op jit(solution)/shard_map/ppermute | solution.py:971
  89.7 1.0 shard_map.151
  90.7 1.6 %collective-permute-start.10 = (bf16[520,256]{1,0:T(8,128)(2,1)S(1)}, bf16[520,256]{1,0:T(8,128)(2,1)S(1)}, u32[]{:S(2)}, u32[]{:S(2)}) collective-permute-start(bf16[520,256]{1,0:T(8,128)(2,1)S(1)} %get-tuple-element.108), channel_id=1, source_target_pairs={{0,1},{1,0},{2,3},{3,2},{4,5},{5,4},{6,7},{7,6},{8,9},{9,8},{10,11... | collective-permute-start | bytes 798728 | tf_op jit(solution)/shard_map/ppermute | solution.py:812
  92.3 2.6 %shard_map.149 = (bf16[1024,256]{1,0:T(8,128)(2,1)}, bf16[1024,1024]{1,0:T(8,128)(2,1)S(1)}, f32[1024,256]{1,0:T(8,128)S(1)}, f32[1024,256]{1,0:T(8,128)S(1)}, f32[1024,256]{1,0:T(8,128)S(1)}) custom-call(s32[8,128]{1,0:T(8,128)S(1)} %copy-done.15, s32[1,1024]{1,0:T(1,128)S(1)} %bitcast.8, bf16[1024,512]{1,0:T(8,128)(2,1)S(1)} %get-tuple-element.62.ordered_ref, ...), custom_call_target="tpu_custom_call" | custom-call | flops 1000 | bytes 1000 | tf_op jit(solution)/shard_map/pallas_call | solution.py:1016
  94.9 2.9 %collective-permute-done.10.refs_0_ = bf16[520,256]{1,0:T(8,128)(2,1)S(1)} collective-permute-done((bf16[520,256]{1,0:T(8,128)(2,1)S(1)}, bf16[520,256]{1,0:T(8,128)(2,1)S(1)}, u32[]{:S(2)}, u32[]{:S(2)}) %collective-permute-start.10) | collective-permute-done | bytes 266272 | tf_op jit(solution)/shard_map/ppermute | solution.py:812
  97.8 2.4 %shard_map.153 = f32[1024,256]{1,0:T(8,128)} custom-call(bf16[1024,1024]{1,0:T(8,128)(2,1)S(1)} %get-tuple-element.93.matrix_ref, f32[1024,256]{1,0:T(8,128)S(1)} %get-tuple-element.94.base_ref, f32[1024,256]{1,0:T(8,128)S(1)} %get-tuple-element.95.scale_ref, f32[1024,256]{1,0:T(8,128)S(1)} %get-tuple-element.96.norm_ref, ...), custom_call_target="tpu_custom_call" | custom-call | flops 1000 | bytes 1000 | tf_op jit(solution)/shard_map/pallas_call | solution.py:1022
  (37 shorter events, 0.2 us)
Async XLA Ops:
  0.6 9.3 %copy-start.8 = (bf16[256,512]{1,0:T(8,128)(2,1)S(1)}, bf16[256,512]{1,0:T(8,128)(2,1)}, u32[]{:S(2)}) copy-start(bf16[256,512]{1,0:T(8,128)(2,1)} %wo_ref.3) | copy-start | bytes 786436
  0.6 9.4 %copy-start.9 = (bf16[512,256]{1,0:T(8,128)(2,1)S(1)}, bf16[512,256]{1,0:T(8,128)(2,1)}, u32[]{:S(2)}) copy-start(bf16[512,256]{1,0:T(8,128)(2,1)} %wq_ref.3) | copy-start | bytes 786436
  0.7 9.4 %copy-start.2 = (bf16[512,256]{1,0:T(8,128)(2,1)S(1)}, bf16[512,256]{1,0:T(8,128)(2,1)}, u32[]{:S(2)}) copy-start(bf16[512,256]{1,0:T(8,128)(2,1)} %wv_ref.9) | copy-start | bytes 786436
  0.7 9.4 %copy-start.1 = (bf16[512,256]{1,0:T(8,128)(2,1)S(1)}, bf16[512,256]{1,0:T(8,128)(2,1)}, u32[]{:S(2)}) copy-start(bf16[512,256]{1,0:T(8,128)(2,1)} %wk_ref.9) | copy-start | bytes 786436
  0.7 11.9 %copy-start.6 = (bf16[1024,512]{1,0:T(8,128)(2,1)S(1)}, bf16[1024,512]{1,0:T(8,128)(2,1)}, u32[]{:S(2)}) copy-start(bf16[1024,512]{1,0:T(8,128)(2,1)} %out_ref.1) | copy-start | bytes 3145732
  4.5 8.1 %copy-start.4 = (bf16[512,1024]{1,0:T(8,128)(2,1)S(1)}, bf16[512,1024]{1,0:T(8,128)(2,1)}, u32[]{:S(2)}) copy-start(bf16[512,1024]{1,0:T(8,128)(2,1)} %in_ref.1) | copy-start | bytes 3145732
  4.5 32.2 %collective-permute-start.2 = (bf16[1024,512]{1,0:T(8,128)(2,1)}, bf16[1024,512]{1,0:T(8,128)(2,1)}, u32[]{:S(2)}, u32[]{:S(2)}) collective-permute-start(bf16[1024,512]{1,0:T(8,128)(2,1)} %shard_map.140.own_ref.normed_ref), channel_id=1, source_target_pairs={{2,0},{4,2},{6,4},{8,6},{10,8},{12,10},{14,12},{16,14},{18,16},{20... | collective-permute-start | bytes 3145736 | tf_op jit(solution)/shard_map/ppermute | solution.py:822
  9.9 26.8 %collective-permute-start.1 = (bf16[1024,512]{1,0:T(8,128)(2,1)}, bf16[1024,512]{1,0:T(8,128)(2,1)}, u32[]{:S(2)}, u32[]{:S(2)}) collective-permute-start(bf16[1024,512]{1,0:T(8,128)(2,1)} %shard_map.140.own_ref.normed_ref), channel_id=1, source_target_pairs={{0,2},{2,4},{4,6},{6,8},{8,10},{10,12},{12,14},{14,16},{16,18},{18... | collective-permute-start | bytes 3145736 | tf_op jit(solution)/shard_map/ppermute | solution.py:821
  11.0 15.1 %collective-permute-start = (bf16[512,512]{1,0:T(8,128)(2,1)}, bf16[512,512]{1,0:T(8,128)(2,1)S(1)}, u32[]{:S(2)}, u32[]{:S(2)}) collective-permute-start(bf16[512,512]{1,0:T(8,128)(2,1)} %pad_maximum_fusion.1), channel_id=1, source_target_pairs={{0,1},{1,0},{2,3},{3,2},{4,5},{5,4},{6,7},{7,6},{8,9},{9,8},{10,11... | collective-permute-start | bytes 1572872 | tf_op jit(solution)/shard_map/ppermute | solution.py:812
  12.5 1.7 %copy-start.3 = (bf16[1024,512]{1,0:T(8,128)(2,1)S(1)}, bf16[1024,512]{1,0:T(8,128)(2,1)}, u32[]{:S(2)}) copy-start(bf16[1024,512]{1,0:T(8,128)(2,1)} %rows_ref.3) | copy-start | bytes 3145732
  12.5 1.9 %copy-start.14 = (bf16[1024,512]{1,0:T(8,128)(2,1)S(1)}, bf16[1024,512]{1,0:T(8,128)(2,1)}, u32[]{:S(2)}) copy-start(bf16[1024,512]{1,0:T(8,128)(2,1)} %grads_ref.1) | copy-start | bytes 3145732
  12.5 1.9 %copy-start.16 = (s32[1024]{0:T(1024)S(1)}, s32[1024]{0:T(1024)}, u32[]{:S(2)}) copy-start(s32[1024]{0:T(1024)} %param.15) | copy-start | bytes 12292
  12.6 15.3 %copy-start = (bf16[1024,512]{1,0:T(8,128)(2,1)S(1)}, bf16[1024,512]{1,0:T(8,128)(2,1)}, u32[]{:S(2)}) copy-start(bf16[1024,512]{1,0:T(8,128)(2,1)} %shard_map.140.own_ref.normed_ref) | copy-start | bytes 3145732
  13.7 31.7 %collective-permute-start.4 = (bf16[1024,512]{1,0:T(8,128)(2,1)}, bf16[1024,512]{1,0:T(8,128)(2,1)}, u32[]{:S(2)}, u32[]{:S(2)}) collective-permute-start(bf16[1024,512]{1,0:T(8,128)(2,1)} %pad_maximum_fusion), channel_id=1, source_target_pairs={{0,1},{1,0},{2,3},{3,2},{4,5},{5,4},{6,7},{7,6},{8,9},{9,8},{10,11... | collective-permute-start | bytes 3145736 | tf_op jit(solution)/shard_map/ppermute | solution.py:812
  16.8 1.0 copy-start.12
  26.1 1.9 %collective-permute-start.3 = (bf16[512,512]{1,0:T(8,128)(2,1)S(1)}, bf16[512,512]{1,0:T(8,128)(2,1)S(1)}, u32[]{:S(2)}, u32[]{:S(2)}) collective-permute-start(bf16[512,512]{1,0:T(8,128)(2,1)S(1)} %collective-permute-done.pack_a), channel_id=1, source_target_pairs={{0,2},{2,0},{4,6},{6,4},{8,10},{10,8},{12,14},{14,12},{16,18},{18,... | collective-permute-start | bytes 1572872 | tf_op jit(solution)/shard_map/ppermute | solution.py:851
  28.0 1.0 copy-start.10
  28.9 0.7 copy-start.15
  36.7 9.7 %copy-start.5 = (bf16[512,1024]{1,0:T(8,128)(2,1)S(1)}, bf16[512,1024]{1,0:T(8,128)(2,1)}, u32[]{:S(2)}) copy-start(bf16[512,1024]{1,0:T(8,128)(2,1)} %in_ref.1) | copy-start | bytes 3145732
  36.7 9.7 %copy-start.7 = (bf16[1024,512]{1,0:T(8,128)(2,1)S(1)}, bf16[1024,512]{1,0:T(8,128)(2,1)}, u32[]{:S(2)}) copy-start(bf16[1024,512]{1,0:T(8,128)(2,1)} %out_ref.1) | copy-start | bytes 3145732
  36.7 9.7 %copy-start.13 = (bf16[1024,512]{1,0:T(8,128)(2,1)S(1)}, bf16[1024,512]{1,0:T(8,128)(2,1)}, u32[]{:S(2)}) copy-start(bf16[1024,512]{1,0:T(8,128)(2,1)} %copy-done.12) | copy-start | bytes 3145732
  36.7 9.7 %copy-start.18 = (f32[512]{0:T(512)S(1)}, f32[512]{0:T(512)}, u32[]{:S(2)}) copy-start(f32[512]{0:T(512)} %param.23) | copy-start | bytes 6148
  45.4 4.8 %collective-permute-start.5 = (bf16[1024,512]{1,0:T(8,128)(2,1)}, bf16[1024,512]{1,0:T(8,128)(2,1)S(1)}, u32[]{:S(2)}, u32[]{:S(2)}) collective-permute-start(bf16[1024,512]{1,0:T(8,128)(2,1)} %collective-permute-done.4.hidden_a), channel_id=1, source_target_pairs={{0,2},{2,0},{4,6},{6,4},{8,10},{10,8},{12,14},{14,12},{16,18},{18,... | collective-permute-start | bytes 3145736 | tf_op jit(solution)/shard_map/ppermute | solution.py:917
  62.4 22.2 %collective-permute-start.7 = (bf16[1024,512]{1,0:T(8,128)(2,1)S(1)}, bf16[1024,512]{1,0:T(8,128)(2,1)S(1)}, u32[]{:S(2)}, u32[]{:S(2)}) collective-permute-start(bf16[1024,512]{1,0:T(8,128)(2,1)S(1)} %get-tuple-element.101), channel_id=1, source_target_pairs={{2,0},{4,2},{6,4},{8,6},{10,8},{12,10},{14,12},{16,14},{18,16},{20... | collective-permute-start | bytes 3145736 | tf_op jit(solution)/shard_map/ppermute | solution.py:969
  65.8 10.9 %collective-permute-start.6 = (bf16[512,512]{1,0:T(8,128)(2,1)S(1)}, bf16[512,512]{1,0:T(8,128)(2,1)S(1)}, u32[]{:S(2)}, u32[]{:S(2)}) collective-permute-start(bf16[512,512]{1,0:T(8,128)(2,1)S(1)} %get-tuple-element.90), channel_id=1, source_target_pairs={{0,1},{1,0},{2,3},{3,2},{4,5},{5,4},{6,7},{7,6},{8,9},{9,8},{10,11... | collective-permute-start | bytes 1572872 | tf_op jit(solution)/shard_map/ppermute | solution.py:812
  66.6 10.2 %copy-start.11 = (bf16[512,256]{1,0:T(8,128)(2,1)S(1)}, bf16[512,256]{1,0:T(8,128)(2,1)}, u32[]{:S(2)}) copy-start(bf16[512,256]{1,0:T(8,128)(2,1)} %wq_ref.3) | copy-start | bytes 786436
  72.7 11.9 %collective-permute-start.9 = (bf16[512,512]{1,0:T(8,128)(2,1)S(1)}, bf16[512,512]{1,0:T(8,128)(2,1)S(1)}, u32[]{:S(2)}, u32[]{:S(2)}) collective-permute-start(bf16[512,512]{1,0:T(8,128)(2,1)S(1)} %get-tuple-element.105), channel_id=1, source_target_pairs={{0,2},{2,4},{4,6},{6,8},{8,10},{10,12},{12,14},{14,16},{16,18},{18... | collective-permute-start | bytes 1572872 | tf_op jit(solution)/shard_map/ppermute | solution.py:971
  72.8 16.9 %collective-permute-start.8 = (bf16[512,512]{1,0:T(8,128)(2,1)S(1)}, bf16[512,512]{1,0:T(8,128)(2,1)S(1)}, u32[]{:S(2)}, u32[]{:S(2)}) collective-permute-start(bf16[512,512]{1,0:T(8,128)(2,1)S(1)} %get-tuple-element.102), channel_id=1, source_target_pairs={{0,2},{2,4},{4,6},{6,8},{8,10},{10,12},{12,14},{14,16},{16,18},{18... | collective-permute-start | bytes 1572872 | tf_op jit(solution)/shard_map/ppermute | solution.py:971
  85.6 6.7 %copy-start.17 = (f32[512]{0:T(512)S(1)}, f32[512]{0:T(512)}, u32[]{:S(2)}) copy-start(f32[512]{0:T(512)} %param.18) | copy-start | bytes 6148
  85.6 9.3 %collective-permute-start.11 = (bf16[520,256]{1,0:T(8,128)(2,1)S(1)}, bf16[520,256]{1,0:T(8,128)(2,1)S(1)}, u32[]{:S(2)}, u32[]{:S(2)}) collective-permute-start(bf16[520,256]{1,0:T(8,128)(2,1)S(1)} %get-tuple-element.109), channel_id=1, source_target_pairs={{0,1},{1,0},{2,3},{3,2},{4,5},{5,4},{6,7},{7,6},{8,9},{9,8},{10,11... | collective-permute-start | bytes 798728 | tf_op jit(solution)/shard_map/ppermute | solution.py:812
  90.7 7.1 %collective-permute-start.10 = (bf16[520,256]{1,0:T(8,128)(2,1)S(1)}, bf16[520,256]{1,0:T(8,128)(2,1)S(1)}, u32[]{:S(2)}, u32[]{:S(2)}) collective-permute-start(bf16[520,256]{1,0:T(8,128)(2,1)S(1)} %get-tuple-element.108), channel_id=1, source_target_pairs={{0,1},{1,0},{2,3},{3,2},{4,5},{5,4},{6,7},{7,6},{8,9},{9,8},{10,11... | collective-permute-start | bytes 798728 | tf_op jit(solution)/shard_map/ppermute | solution.py:812
